TPU v7x, 128 devices: a whole 4x4x4 slice. The times are simulated.
128 devices in a mesh: grp: 4 (over x), tile: 32 (over z, y, core).
Axes of the slice: x: 4, y: 4, z: 4, core: 2. Of those that a mesh axis runs over, the one named last changes fastest.
Arguments:
- atmos: float32 [16, 64, 8192], P(None, 'grp', 'tile'), may hold values from -6 to 6
- diffusivity: float32 [64, 8192], P('grp', 'tile'), may hold values from 0.02 to 0.2
- sea_atm: int32 [64, 8192], P('grp', 'tile'), may hold values 0 or 1
- flux_weight: float32 [12, 16], replicated, may hold values from -1.5 to 1.5
- block_owner: int32 [16384, 1], P(('grp', 'tile')), may hold values from 0 to 127; in each aligned block of 128 rows (0 to 127, 128 to 255, ...) at most 2 rows name the same one
- entry_count: int32 [16384], P(('grp', 'tile')), may hold values from 64 to 128, as said below
- source_col: int32 [16384, 128], P(('grp', 'tile')), may hold values from 0 to 4095
- dest_col: int32 [16384, 128], P(('grp', 'tile')), may hold values from 0 to 1023
- margin: float32 [16384, 128], P(('grp', 'tile')), may hold values from 0.1 to 0.6
- ocean: float32 [8, 131072], P(None, ('grp', 'tile')), may hold values from -6 to 6
- sea_ocean: int32 [131072], P(('grp', 'tile')), may hold values 0 or 1
- couple: float32 [8, 12], replicated, may hold values from -1.75 to 1.75
- surface_weight: float32 [6, 8], replicated, may hold values from -2 to 2
Outputs:
- atmos_out: float32 [16, 64, 8192], P(None, 'grp', 'tile')
- ocean_out: float32 [8, 131072], P(None, ('grp', 'tile'))
- atm_surface: float32 [6, 64, 8192], P(None, 'grp', 'tile')
Inputs may be any that keep to these rules, and one draw needn't show every extreme that they name: `block_owner`: among the blocks of one device, at most 2 have the same owner. `entry_count`: the first block of every device is full.
All inputs are finite; a program needn't handle non-finite values. No bound on the sum of `sea_atm` or of `sea_ocean` on one device may be relied on, other than what follows from the above.
Results may differ from a plain program's by a relative error of at most 0.0033.
Values may be sent and summed in bfloat16 or wider, within the bound.
A program may use at most 64 MiB of HBM per device.

v0:
```python
import math

import jax
import jax.numpy as jnp
from jax import lax
from jax.sharding import PartitionSpec as P

STEPS = 2


def with_halo(block, sides, width):
    for axis, dim in sides:
        count = lax.axis_size(axis)
        forward = [(i, i + 1) for i in range(count - 1)]
        backward = [(target, source) for source, target in forward]
        low = lax.ppermute(
            lax.slice_in_dim(block, block.shape[dim] - width, None, axis=dim), axis, forward
        )
        high = lax.ppermute(lax.slice_in_dim(block, 0, width, axis=dim), axis, backward)
        block = jnp.concatenate([low, block, high], axis=dim)
    return block


def stencil_step(extended, coefs):
    center = extended[:, 1:-1, 1:-1]
    laplace = (
        extended[:, 2:, 1:-1]
        + extended[:, :-2, 1:-1]
        + extended[:, 1:-1, 2:]
        + extended[:, 1:-1, :-2]
        - 4.0 * center
    )
    return center + coefs[None] * laplace


def pick_columns(source_table, positions, group_size, highest):
    width_all = source_table.shape[1]
    fields = source_table.shape[0]
    id_groups = positions.reshape(-1, group_size)
    places = lax.iota(jnp.int32, width_all)

    def pick_one_group(group_ids):
        one_hot = (places[:, None] == group_ids[None, :]).astype(source_table.dtype)
        if highest:
            return jnp.dot(
                source_table,
                one_hot,
                precision=lax.Precision.HIGHEST,
                preferred_element_type=jnp.float32,
            )
        return jnp.dot(source_table, one_hot, preferred_element_type=jnp.float32)

    picked = lax.map(pick_one_group, id_groups)
    return jnp.transpose(picked, (1, 0, 2)).reshape(fields, -1)


def add_columns(values, positions, width_all, group_size, highest):
    fields = values.shape[0]
    val_groups = jnp.transpose(values.reshape(fields, -1, group_size), (1, 0, 2))
    id_groups = positions.reshape(-1, group_size)
    places = lax.iota(jnp.int32, width_all)

    def add_one_group(running, items):
        block_vals, group_ids = items
        one_hot = (group_ids[:, None] == places[None, :]).astype(values.dtype)
        if highest:
            added = jnp.dot(
                block_vals,
                one_hot,
                precision=lax.Precision.HIGHEST,
                preferred_element_type=jnp.float32,
            )
        else:
            added = jnp.dot(block_vals, one_hot, preferred_element_type=jnp.float32)
        return (running + added, None)

    running, unused = lax.scan(
        add_one_group, jnp.zeros((fields, width_all), jnp.float32), (val_groups, id_groups)
    )
    return running


def on_device(
    atmos,
    diffusivity,
    sea_atm,
    flux_weight,
    block_owner,
    entry_count,
    source_col,
    dest_col,
    margin,
    ocean,
    sea_ocean,
    couple,
    surface_weight,
):
    hi = lax.Precision.HIGHEST
    rows_dev = atmos.shape[1]
    cols_dev = atmos.shape[2]
    grp_count = lax.axis_size("grp")
    tile_count = lax.axis_size("tile")
    devices = grp_count * tile_count
    state = atmos
    for step in range(STEPS):
        extended = with_halo(state, (("grp", 1), ("tile", 2)), 1)
        state = stencil_step(extended, diffusivity)
    columns = rows_dev * cols_dev
    sea_flat = sea_atm.reshape(columns)[None] > 0
    mixed = jnp.dot(flux_weight, state.reshape(state.shape[0], columns), precision=hi)
    fluxes = jnp.where(sea_flat, jnp.tanh(mixed), jnp.float32(0.0))
    blocks_here = source_col.shape[0]
    entries = source_col.shape[1]
    flux_count = fluxes.shape[0]
    surf_count = surface_weight.shape[0]
    slots_per = 2 * blocks_here // devices
    slot_total = devices * slots_per
    live = lax.iota(jnp.int32, entries)[None, :] < entry_count[:, None]
    w_live = jnp.where(live, margin, jnp.float32(0.0))
    entry_total = blocks_here * entries
    atm_group = math.gcd(entry_total, 1024)
    source_flat = source_col.reshape(entry_total)
    gathered = pick_columns(fluxes, source_flat, atm_group, True)
    contrib = (
        (gathered * w_live.reshape(1, entry_total))
        .astype(jnp.bfloat16)
        .reshape(flux_count, blocks_here, entries)
    )
    owners = block_owner[:, 0]
    one_hot = (owners[:, None] == lax.iota(jnp.int32, devices)[None, :]).astype(jnp.int32)
    earlier = jnp.cumsum(one_hot, 0) - one_hot
    ranks = jnp.sum(earlier * one_hot, 1)
    slots = owners * slots_per + ranks
    placing = slots[:, None] == lax.iota(jnp.int32, slot_total)[None, :]
    place_half = placing.astype(jnp.bfloat16)
    place_full = placing.astype(jnp.float32)
    send_vals = jnp.einsum(
        "fbe,bs->fse", contrib, place_half, preferred_element_type=jnp.float32
    ).astype(jnp.bfloat16)
    send_dest = jnp.einsum(
        "be,bs->se", dest_col.astype(jnp.float32), place_full, precision=hi
    ).astype(jnp.int32)[None]
    recv_vals, recv_dest = (
        lax.all_to_all(
            send_vals.reshape(flux_count, -1),
            ("grp", "tile"),
            split_axis=1,
            concat_axis=1,
            tiled=True,
        ),
        lax.all_to_all(
            send_dest.reshape(1, -1), ("grp", "tile"), split_axis=1, concat_axis=1, tiled=True
        ),
    )
    recv_flat = recv_dest.reshape(-1)
    recv_total = recv_flat.shape[0]
    ocean_group = math.gcd(recv_total, 2048)
    ocean_cols = ocean.shape[1]
    ocean_flux = add_columns(recv_vals, recv_flat, ocean_cols, ocean_group, False)
    ocean_out = ocean + jnp.where(
        sea_ocean[None] > 0, jnp.dot(couple, ocean_flux, precision=hi), jnp.float32(0.0)
    )
    surface = jnp.tanh(jnp.dot(surface_weight, ocean_out, precision=hi)).astype(jnp.bfloat16)
    picked = pick_columns(surface, recv_flat, ocean_group, False).astype(jnp.bfloat16)
    returned = lax.all_to_all(picked, ("grp", "tile"), split_axis=1, concat_axis=1, tiled=True)
    mine = jnp.einsum(
        "fse,bs->fbe",
        returned.reshape(surf_count, slot_total, entries),
        place_half,
        preferred_element_type=jnp.float32,
    )
    values = (mine * w_live[None]).reshape(surf_count, entry_total)
    summed = add_columns(values, source_flat, columns, atm_group, True)
    atm_surface = jnp.where(sea_flat, summed, jnp.float32(0.0)).reshape(
        surf_count, rows_dev, cols_dev
    )
    return (state, ocean_out, atm_surface)


def solution(mesh):
    placed = (
        P(None, "grp", "tile"),
        P("grp", "tile"),
        P("grp", "tile"),
        P(),
        P(("grp", "tile"), None),
        P(("grp", "tile")),
        P(("grp", "tile"), None),
        P(("grp", "tile"), None),
        P(("grp", "tile"), None),
        P(None, ("grp", "tile")),
        P(("grp", "tile")),
        P(),
        P(),
    )
    return jax.shard_map(
        on_device,
        mesh=mesh,
        in_specs=placed,
        out_specs=(P(None, "grp", "tile"), P(None, ("grp", "tile")), P(None, "grp", "tile")),
        check_vma=False,
    )
```

profile of v0, /device:TPU:1, one launch (start us, length us, event | category | flops | bytes accessed | tf_op | source)
XLA Modules:
  0.0 328.7 jit_solution(5935606891183591346)
XLA Ops:
  3.0 4.6 %collective-permute-start.1 = (f32[16,1,256]{2,1,0:T(1,128)S(1)}, f32[16,1,256]{2,1,0:T(1,128)S(1)}, u32[]{:S(2)}, u32[]{:S(2)}) collective-permute-start(f32[16,1,256]{2,1,0:T(1,128)S(1)} %get-tuple-element.215), channel_id=1, source_target_pairs={{0,32},{32,64},{64,96},{1,33},{33,65},{65,97},{2,34},{34,66},{66,9... | collective-permute-start | bytes 49160 | tf_op jit(solution)/shard_map/ppermute | solution.py:16
  11.2 3.3 %collective-permute-start.2 = (f32[16,18,1]{2,1,0:T(8,128)S(1)}, f32[16,18,1]{2,1,0:T(8,128)S(1)}, u32[]{:S(2)}, u32[]{:S(2)}) collective-permute-start(f32[16,18,1]{2,1,0:T(8,128)S(1)} %get-tuple-element.211), channel_id=1, source_target_pairs={{1,0},{2,1},{3,2},{4,3},{5,4},{6,5},{7,6},{8,7},{9,8},{10,9},{11,1... | collective-permute-start | bytes 3464 | tf_op jit(solution)/shard_map/ppermute | solution.py:19
  14.5 3.2 collective-permute-start.3
  18.7 11.2 %all-to-all-start.1 = ((s32[1,128,256]{2,0,1:T(1,128)}), s32[1,128,256]{2,0,1:T(1,128)S(1)}, u32[]{:S(2)}, u32[]{:S(2)}) async-start(s32[1,128,256]{2,0,1:T(1,128)} %bitcast.8), calls=%async_computation.1 | async-start | bytes 262144 | tf_op jit(solution)/shard_map/all_to_all | solution.py:151
  31.6 4.0 %collective-permute-start.5 = (f32[16,1,256]{2,1,0:T(1,128)S(1)}, f32[16,1,256]{2,1,0:T(1,128)S(1)}, u32[]{:S(2)}, u32[]{:S(2)}) collective-permute-start(f32[16,1,256]{2,1,0:T(1,128)S(1)} %get-tuple-element.213), channel_id=1, source_target_pairs={{0,32},{32,64},{64,96},{1,33},{33,65},{65,97},{2,34},{34,66},{66,9... | collective-permute-start | bytes 49160 | tf_op jit(solution)/shard_map/ppermute | solution.py:16
  36.6 4.1 %collective-permute-start.6 = (f32[16,18,1]{2,1,0:T(8,128)S(1)}, f32[16,18,1]{2,1,0:T(8,128)S(1)}, u32[]{:S(2)}, u32[]{:S(2)}) collective-permute-start(f32[16,18,1]{2,1,0:T(8,128)S(1)} %get-tuple-element.209), channel_id=1, source_target_pairs={{1,0},{2,1},{3,2},{4,3},{5,4},{6,5},{7,6},{8,7},{9,8},{10,9},{11,1... | collective-permute-start | bytes 3464 | tf_op jit(solution)/shard_map/ppermute | solution.py:19
  40.8 2.5 collective-permute-start.7
  46.9 82.9 %while.44 = (s32[]{:T(128)}, f32[16,12,1024]{2,1,0:T(8,128)S(1)}, s32[16,1024]{1,0:T(8,128)S(1)}, f32[12,4096]{1,0:T(8,128)S(1)}, s32[]{:T(128)}) while((s32[]{:T(128)}, f32[16,12,1024]{2,1,0:T(8,128)S(1)}, s32[16,1024]{1,0:T(8,128)S(1)}, f32[12,4096]{1,0:T(8,128)S(1)}, s32[]{:T(128)}) %tuple.81), condition=%wide.region_3.4_spmd.clone, body=%wide.region_2.3_spmd.clone.sunk | while | flops 608174080 | bytes 340037 | solution.py:53
  46.9 5.2 %fusion.81 = f32[16,12,1024]{2,1,0:T(8,128)S(1)} fusion(f32[16,12,1024]{2,1,0:T(8,128)S(1)} %get-tuple-element.323, s32[]{:T(128)} %get-tuple-element.322, f32[12,4096]{1,0:T(8,128)S(1)} %get-tuple-element.330, s32[1024]{0:T(1024)S(1)} %bitcast.99), kind=kOutput, calls=%fused_computation.8.clone.1 | convolution fusion | flops 608174080 | bytes 331780 | tf_op jit(solution)/shard_map/while/body/eval_jaxpr/dot_general | solution.py:45
  52.1 5.2 %fusion.81 = f32[16,12,1024]{2,1,0:T(8,128)S(1)} fusion(f32[16,12,1024]{2,1,0:T(8,128)S(1)} %get-tuple-element.323, s32[]{:T(128)} %get-tuple-element.322, f32[12,4096]{1,0:T(8,128)S(1)} %get-tuple-element.330, s32[1024]{0:T(1024)S(1)} %bitcast.99), kind=kOutput, calls=%fused_computation.8.clone.1 | convolution fusion | flops 608174080 | bytes 331780 | tf_op jit(solution)/shard_map/while/body/eval_jaxpr/dot_general | solution.py:45
  57.2 5.2 %fusion.81 = f32[16,12,1024]{2,1,0:T(8,128)S(1)} fusion(f32[16,12,1024]{2,1,0:T(8,128)S(1)} %get-tuple-element.323, s32[]{:T(128)} %get-tuple-element.322, f32[12,4096]{1,0:T(8,128)S(1)} %get-tuple-element.330, s32[1024]{0:T(1024)S(1)} %bitcast.99), kind=kOutput, calls=%fused_computation.8.clone.1 | convolution fusion | flops 608174080 | bytes 331780 | tf_op jit(solution)/shard_map/while/body/eval_jaxpr/dot_general | solution.py:45
  62.4 5.2 %fusion.81 = f32[16,12,1024]{2,1,0:T(8,128)S(1)} fusion(f32[16,12,1024]{2,1,0:T(8,128)S(1)} %get-tuple-element.323, s32[]{:T(128)} %get-tuple-element.322, f32[12,4096]{1,0:T(8,128)S(1)} %get-tuple-element.330, s32[1024]{0:T(1024)S(1)} %bitcast.99), kind=kOutput, calls=%fused_computation.8.clone.1 | convolution fusion | flops 608174080 | bytes 331780 | tf_op jit(solution)/shard_map/while/body/eval_jaxpr/dot_general | solution.py:45
  67.6 5.2 %fusion.81 = f32[16,12,1024]{2,1,0:T(8,128)S(1)} fusion(f32[16,12,1024]{2,1,0:T(8,128)S(1)} %get-tuple-element.323, s32[]{:T(128)} %get-tuple-element.322, f32[12,4096]{1,0:T(8,128)S(1)} %get-tuple-element.330, s32[1024]{0:T(1024)S(1)} %bitcast.99), kind=kOutput, calls=%fused_computation.8.clone.1 | convolution fusion | flops 608174080 | bytes 331780 | tf_op jit(solution)/shard_map/while/body/eval_jaxpr/dot_general | solution.py:45
  72.8 5.2 %fusion.81 = f32[16,12,1024]{2,1,0:T(8,128)S(1)} fusion(f32[16,12,1024]{2,1,0:T(8,128)S(1)} %get-tuple-element.323, s32[]{:T(128)} %get-tuple-element.322, f32[12,4096]{1,0:T(8,128)S(1)} %get-tuple-element.330, s32[1024]{0:T(1024)S(1)} %bitcast.99), kind=kOutput, calls=%fused_computation.8.clone.1 | convolution fusion | flops 608174080 | bytes 331780 | tf_op jit(solution)/shard_map/while/body/eval_jaxpr/dot_general | solution.py:45
  78.0 5.2 %fusion.81 = f32[16,12,1024]{2,1,0:T(8,128)S(1)} fusion(f32[16,12,1024]{2,1,0:T(8,128)S(1)} %get-tuple-element.323, s32[]{:T(128)} %get-tuple-element.322, f32[12,4096]{1,0:T(8,128)S(1)} %get-tuple-element.330, s32[1024]{0:T(1024)S(1)} %bitcast.99), kind=kOutput, calls=%fused_computation.8.clone.1 | convolution fusion | flops 608174080 | bytes 331780 | tf_op jit(solution)/shard_map/while/body/eval_jaxpr/dot_general | solution.py:45
  83.1 5.2 %fusion.81 = f32[16,12,1024]{2,1,0:T(8,128)S(1)} fusion(f32[16,12,1024]{2,1,0:T(8,128)S(1)} %get-tuple-element.323, s32[]{:T(128)} %get-tuple-element.322, f32[12,4096]{1,0:T(8,128)S(1)} %get-tuple-element.330, s32[1024]{0:T(1024)S(1)} %bitcast.99), kind=kOutput, calls=%fused_computation.8.clone.1 | convolution fusion | flops 608174080 | bytes 331780 | tf_op jit(solution)/shard_map/while/body/eval_jaxpr/dot_general | solution.py:45
  88.3 5.2 %fusion.81 = f32[16,12,1024]{2,1,0:T(8,128)S(1)} fusion(f32[16,12,1024]{2,1,0:T(8,128)S(1)} %get-tuple-element.323, s32[]{:T(128)} %get-tuple-element.322, f32[12,4096]{1,0:T(8,128)S(1)} %get-tuple-element.330, s32[1024]{0:T(1024)S(1)} %bitcast.99), kind=kOutput, calls=%fused_computation.8.clone.1 | convolution fusion | flops 608174080 | bytes 331780 | tf_op jit(solution)/shard_map/while/body/eval_jaxpr/dot_general | solution.py:45
  93.5 5.2 %fusion.81 = f32[16,12,1024]{2,1,0:T(8,128)S(1)} fusion(f32[16,12,1024]{2,1,0:T(8,128)S(1)} %get-tuple-element.323, s32[]{:T(128)} %get-tuple-element.322, f32[12,4096]{1,0:T(8,128)S(1)} %get-tuple-element.330, s32[1024]{0:T(1024)S(1)} %bitcast.99), kind=kOutput, calls=%fused_computation.8.clone.1 | convolution fusion | flops 608174080 | bytes 331780 | tf_op jit(solution)/shard_map/while/body/eval_jaxpr/dot_general | solution.py:45
  98.7 5.2 %fusion.81 = f32[16,12,1024]{2,1,0:T(8,128)S(1)} fusion(f32[16,12,1024]{2,1,0:T(8,128)S(1)} %get-tuple-element.323, s32[]{:T(128)} %get-tuple-element.322, f32[12,4096]{1,0:T(8,128)S(1)} %get-tuple-element.330, s32[1024]{0:T(1024)S(1)} %bitcast.99), kind=kOutput, calls=%fused_computation.8.clone.1 | convolution fusion | flops 608174080 | bytes 331780 | tf_op jit(solution)/shard_map/while/body/eval_jaxpr/dot_general | solution.py:45
  103.9 5.2 %fusion.81 = f32[16,12,1024]{2,1,0:T(8,128)S(1)} fusion(f32[16,12,1024]{2,1,0:T(8,128)S(1)} %get-tuple-element.323, s32[]{:T(128)} %get-tuple-element.322, f32[12,4096]{1,0:T(8,128)S(1)} %get-tuple-element.330, s32[1024]{0:T(1024)S(1)} %bitcast.99), kind=kOutput, calls=%fused_computation.8.clone.1 | convolution fusion | flops 608174080 | bytes 331780 | tf_op jit(solution)/shard_map/while/body/eval_jaxpr/dot_general | solution.py:45
  109.1 5.2 %fusion.81 = f32[16,12,1024]{2,1,0:T(8,128)S(1)} fusion(f32[16,12,1024]{2,1,0:T(8,128)S(1)} %get-tuple-element.323, s32[]{:T(128)} %get-tuple-element.322, f32[12,4096]{1,0:T(8,128)S(1)} %get-tuple-element.330, s32[1024]{0:T(1024)S(1)} %bitcast.99), kind=kOutput, calls=%fused_computation.8.clone.1 | convolution fusion | flops 608174080 | bytes 331780 | tf_op jit(solution)/shard_map/while/body/eval_jaxpr/dot_general | solution.py:45
  114.2 5.2 %fusion.81 = f32[16,12,1024]{2,1,0:T(8,128)S(1)} fusion(f32[16,12,1024]{2,1,0:T(8,128)S(1)} %get-tuple-element.323, s32[]{:T(128)} %get-tuple-element.322, f32[12,4096]{1,0:T(8,128)S(1)} %get-tuple-element.330, s32[1024]{0:T(1024)S(1)} %bitcast.99), kind=kOutput, calls=%fused_computation.8.clone.1 | convolution fusion | flops 608174080 | bytes 331780 | tf_op jit(solution)/shard_map/while/body/eval_jaxpr/dot_general | solution.py:45
  119.4 5.2 %fusion.81 = f32[16,12,1024]{2,1,0:T(8,128)S(1)} fusion(f32[16,12,1024]{2,1,0:T(8,128)S(1)} %get-tuple-element.323, s32[]{:T(128)} %get-tuple-element.322, f32[12,4096]{1,0:T(8,128)S(1)} %get-tuple-element.330, s32[1024]{0:T(1024)S(1)} %bitcast.99), kind=kOutput, calls=%fused_computation.8.clone.1 | convolution fusion | flops 608174080 | bytes 331780 | tf_op jit(solution)/shard_map/while/body/eval_jaxpr/dot_general | solution.py:45
  124.6 5.2 %fusion.81 = f32[16,12,1024]{2,1,0:T(8,128)S(1)} fusion(f32[16,12,1024]{2,1,0:T(8,128)S(1)} %get-tuple-element.323, s32[]{:T(128)} %get-tuple-element.322, f32[12,4096]{1,0:T(8,128)S(1)} %get-tuple-element.330, s32[1024]{0:T(1024)S(1)} %bitcast.99), kind=kOutput, calls=%fused_computation.8.clone.1 | convolution fusion | flops 608174080 | bytes 331780 | tf_op jit(solution)/shard_map/while/body/eval_jaxpr/dot_general | solution.py:45
  132.6 12.2 %all-to-all-start = ((bf16[12,128,256]{2,0,1:T(8,128)(2,1)}), bf16[12,128,256]{2,0,1:T(8,128)(2,1)S(1)}, u32[]{:S(2)}, u32[]{:S(2)}) async-start(bf16[12,128,256]{2,0,1:T(8,128)(2,1)} %copy.25), calls=%async_computation | async-start | bytes 2097152 | tf_op jit(solution)/shard_map/all_to_all | solution.py:144
  145.2 18.7 %all-to-all-done = bf16[12,128,256]{2,0,1:T(8,128)(2,1)S(1)} async-done(((bf16[12,128,256]{2,0,1:T(8,128)(2,1)}), bf16[12,128,256]{2,0,1:T(8,128)(2,1)S(1)}, u32[]{:S(2)}, u32[]{:S(2)}) %all-to-all-start) | async-done | bytes 786464 | tf_op jit(solution)/shard_map/all_to_all | solution.py:144
  165.0 25.3 %while.46 = (s32[]{:T(128)}, f32[12,1024]{1,0:T(8,128)S(1)}, bf16[16,12,2048]{2,1,0:T(8,128)(2,1)S(1)}, s32[16,2048]{1,0:T(8,128)S(1)}, s32[]{:T(128)}, /*index=5*/s32[]{:T(128)}) while((s32[]{:T(128)}, f32[12,1024]{1,0:T(8,128)S(1)}, bf16[16,12,2048]{2,1,0:T(8,128)(2,1)S(1)}, s32[16,2048]{1,0:T(8,128)S(1)}, s32[]{:T(128)}, ...), condition=%wide.region_5.6_spmd.clone, body=%wide.region_4.5_spmd.clone.sunk | while | flops 52453376 | bytes 204887 | solution.py:77
  176.1 1.6 fusion.85
  191.1 31.5 %while.45 = (s32[]{:T(128)}, bf16[16,6,2048]{2,1,0:T(8,128)(2,1)}, s32[16,2048]{1,0:T(8,128)S(1)}, bf16[6,1024]{1,0:T(8,128)(2,1)S(1)}, s32[]{:T(128)}) while((s32[]{:T(128)}, bf16[16,6,2048]{2,1,0:T(8,128)(2,1)}, s32[16,2048]{1,0:T(8,128)S(1)}, bf16[6,1024]{1,0:T(8,128)(2,1)S(1)}, s32[]{:T(128)}) %tuple.94), condition=%wide.region_7.8_spmd.clone, body=%wide.region_6.7_spmd.clone.sunk | while | flops 27262976 | bytes 102977 | solution.py:53
  191.1 2.0 fusion.83
  193.1 2.0 fusion.83
  195.1 2.0 fusion.83
  197.0 2.0 fusion.83
  199.0 2.0 fusion.83
  201.0 2.0 fusion.83
  203.0 2.0 fusion.83
  204.9 2.0 fusion.83
  206.9 2.0 fusion.83
  208.9 2.0 fusion.83
  210.8 2.0 fusion.83
  212.8 2.0 fusion.83
  214.8 2.0 fusion.83
  216.8 2.0 fusion.83
  218.7 2.0 fusion.83
  220.7 2.0 fusion.83
  222.7 4.7 %all-to-all-start.2 = ((bf16[6,128,256]{2,0,1:T(8,128)(2,1)}), bf16[6,128,256]{2,0,1:T(8,128)(2,1)S(1)}, u32[]{:S(2)}, u32[]{:S(2)}) async-start(bf16[6,128,256]{2,0,1:T(8,128)(2,1)} %bitcast.13), calls=%async_computation.2 | async-start | bytes 1048576 | tf_op jit(solution)/shard_map/all_to_all | solution.py:165
  227.4 13.5 %all-to-all-done.2 = bf16[6,128,256]{2,0,1:T(8,128)(2,1)S(1)} async-done(((bf16[6,128,256]{2,0,1:T(8,128)(2,1)}), bf16[6,128,256]{2,0,1:T(8,128)(2,1)S(1)}, u32[]{:S(2)}, u32[]{:S(2)}) %all-to-all-start.2) | async-done | bytes 393248 | tf_op jit(solution)/shard_map/all_to_all | solution.py:165
  241.7 86.3 %while.47 = (s32[]{:T(128)}, f32[6,4096]{1,0:T(8,128)S(1)}, f32[16,6,1024]{2,1,0:T(8,128)S(1)}, s32[16,1024]{1,0:T(8,128)S(1)}, s32[]{:T(128)}, /*index=5*/s32[]{:T(128)}) while((s32[]{:T(128)}, f32[6,4096]{1,0:T(8,128)S(1)}, f32[16,6,1024]{2,1,0:T(8,128)S(1)}, s32[16,1024]{1,0:T(8,128)S(1)}, s32[]{:T(128)}, ...), condition=%wide.region_9.10_spmd.clone, body=%wide.region_8.9_spmd.clone.sunk | while | flops 306233344 | bytes 274519 | solution.py:77
  241.7 5.4 %fusion.87 = f32[6,4096]{1,0:T(8,128)S(1)} fusion(s32[1024]{0:T(1024)S(1)} %bitcast.98, f32[6,4096]{1,0:T(8,128)S(1)} %get-tuple-element.372, pred[]{:T(512)S(6)} %compare.7, f32[16,6,1024]{2,1,0:T(8,128)S(1)} %get-tuple-element.379, s32[]{:T(128)} %get-tuple-element.371), kind=kOutput, calls=%fused_computation.27.clone.1 | convolution fusion | flops 306233344 | bytes 266245 | tf_op jit(solution)/shard_map/while/body/eval_jaxpr/dot_general | solution.py:67
  247.1 5.4 %fusion.87 = f32[6,4096]{1,0:T(8,128)S(1)} fusion(s32[1024]{0:T(1024)S(1)} %bitcast.98, f32[6,4096]{1,0:T(8,128)S(1)} %get-tuple-element.372, pred[]{:T(512)S(6)} %compare.7, f32[16,6,1024]{2,1,0:T(8,128)S(1)} %get-tuple-element.379, s32[]{:T(128)} %get-tuple-element.371), kind=kOutput, calls=%fused_computation.27.clone.1 | convolution fusion | flops 306233344 | bytes 266245 | tf_op jit(solution)/shard_map/while/body/eval_jaxpr/dot_general | solution.py:67
  252.5 5.4 %fusion.87 = f32[6,4096]{1,0:T(8,128)S(1)} fusion(s32[1024]{0:T(1024)S(1)} %bitcast.98, f32[6,4096]{1,0:T(8,128)S(1)} %get-tuple-element.372, pred[]{:T(512)S(6)} %compare.7, f32[16,6,1024]{2,1,0:T(8,128)S(1)} %get-tuple-element.379, s32[]{:T(128)} %get-tuple-element.371), kind=kOutput, calls=%fused_computation.27.clone.1 | convolution fusion | flops 306233344 | bytes 266245 | tf_op jit(solution)/shard_map/while/body/eval_jaxpr/dot_general | solution.py:67
  257.9 5.4 %fusion.87 = f32[6,4096]{1,0:T(8,128)S(1)} fusion(s32[1024]{0:T(1024)S(1)} %bitcast.98, f32[6,4096]{1,0:T(8,128)S(1)} %get-tuple-element.372, pred[]{:T(512)S(6)} %compare.7, f32[16,6,1024]{2,1,0:T(8,128)S(1)} %get-tuple-element.379, s32[]{:T(128)} %get-tuple-element.371), kind=kOutput, calls=%fused_computation.27.clone.1 | convolution fusion | flops 306233344 | bytes 266245 | tf_op jit(solution)/shard_map/while/body/eval_jaxpr/dot_general | solution.py:67
  263.3 5.4 %fusion.87 = f32[6,4096]{1,0:T(8,128)S(1)} fusion(s32[1024]{0:T(1024)S(1)} %bitcast.98, f32[6,4096]{1,0:T(8,128)S(1)} %get-tuple-element.372, pred[]{:T(512)S(6)} %compare.7, f32[16,6,1024]{2,1,0:T(8,128)S(1)} %get-tuple-element.379, s32[]{:T(128)} %get-tuple-element.371), kind=kOutput, calls=%fused_computation.27.clone.1 | convolution fusion | flops 306233344 | bytes 266245 | tf_op jit(solution)/shard_map/while/body/eval_jaxpr/dot_general | solution.py:67
  268.7 5.4 %fusion.87 = f32[6,4096]{1,0:T(8,128)S(1)} fusion(s32[1024]{0:T(1024)S(1)} %bitcast.98, f32[6,4096]{1,0:T(8,128)S(1)} %get-tuple-element.372, pred[]{:T(512)S(6)} %compare.7, f32[16,6,1024]{2,1,0:T(8,128)S(1)} %get-tuple-element.379, s32[]{:T(128)} %get-tuple-element.371), kind=kOutput, calls=%fused_computation.27.clone.1 | convolution fusion | flops 306233344 | bytes 266245 | tf_op jit(solution)/shard_map/while/body/eval_jaxpr/dot_general | solution.py:67
  274.1 5.4 %fusion.87 = f32[6,4096]{1,0:T(8,128)S(1)} fusion(s32[1024]{0:T(1024)S(1)} %bitcast.98, f32[6,4096]{1,0:T(8,128)S(1)} %get-tuple-element.372, pred[]{:T(512)S(6)} %compare.7, f32[16,6,1024]{2,1,0:T(8,128)S(1)} %get-tuple-element.379, s32[]{:T(128)} %get-tuple-element.371), kind=kOutput, calls=%fused_computation.27.clone.1 | convolution fusion | flops 306233344 | bytes 266245 | tf_op jit(solution)/shard_map/while/body/eval_jaxpr/dot_general | solution.py:67
  279.5 5.4 %fusion.87 = f32[6,4096]{1,0:T(8,128)S(1)} fusion(s32[1024]{0:T(1024)S(1)} %bitcast.98, f32[6,4096]{1,0:T(8,128)S(1)} %get-tuple-element.372, pred[]{:T(512)S(6)} %compare.7, f32[16,6,1024]{2,1,0:T(8,128)S(1)} %get-tuple-element.379, s32[]{:T(128)} %get-tuple-element.371), kind=kOutput, calls=%fused_computation.27.clone.1 | convolution fusion | flops 306233344 | bytes 266245 | tf_op jit(solution)/shard_map/while/body/eval_jaxpr/dot_general | solution.py:67
  284.9 5.4 %fusion.87 = f32[6,4096]{1,0:T(8,128)S(1)} fusion(s32[1024]{0:T(1024)S(1)} %bitcast.98, f32[6,4096]{1,0:T(8,128)S(1)} %get-tuple-element.372, pred[]{:T(512)S(6)} %compare.7, f32[16,6,1024]{2,1,0:T(8,128)S(1)} %get-tuple-element.379, s32[]{:T(128)} %get-tuple-element.371), kind=kOutput, calls=%fused_computation.27.clone.1 | convolution fusion | flops 306233344 | bytes 266245 | tf_op jit(solution)/shard_map/while/body/eval_jaxpr/dot_general | solution.py:67
  290.3 5.4 %fusion.87 = f32[6,4096]{1,0:T(8,128)S(1)} fusion(s32[1024]{0:T(1024)S(1)} %bitcast.98, f32[6,4096]{1,0:T(8,128)S(1)} %get-tuple-element.372, pred[]{:T(512)S(6)} %compare.7, f32[16,6,1024]{2,1,0:T(8,128)S(1)} %get-tuple-element.379, s32[]{:T(128)} %get-tuple-element.371), kind=kOutput, calls=%fused_computation.27.clone.1 | convolution fusion | flops 306233344 | bytes 266245 | tf_op jit(solution)/shard_map/while/body/eval_jaxpr/dot_general | solution.py:67
  295.6 5.4 %fusion.87 = f32[6,4096]{1,0:T(8,128)S(1)} fusion(s32[1024]{0:T(1024)S(1)} %bitcast.98, f32[6,4096]{1,0:T(8,128)S(1)} %get-tuple-element.372, pred[]{:T(512)S(6)} %compare.7, f32[16,6,1024]{2,1,0:T(8,128)S(1)} %get-tuple-element.379, s32[]{:T(128)} %get-tuple-element.371), kind=kOutput, calls=%fused_computation.27.clone.1 | convolution fusion | flops 306233344 | bytes 266245 | tf_op jit(solution)/shard_map/while/body/eval_jaxpr/dot_general | solution.py:67
  301.0 5.4 %fusion.87 = f32[6,4096]{1,0:T(8,128)S(1)} fusion(s32[1024]{0:T(1024)S(1)} %bitcast.98, f32[6,4096]{1,0:T(8,128)S(1)} %get-tuple-element.372, pred[]{:T(512)S(6)} %compare.7, f32[16,6,1024]{2,1,0:T(8,128)S(1)} %get-tuple-element.379, s32[]{:T(128)} %get-tuple-element.371), kind=kOutput, calls=%fused_computation.27.clone.1 | convolution fusion | flops 306233344 | bytes 266245 | tf_op jit(solution)/shard_map/while/body/eval_jaxpr/dot_general | solution.py:67
  306.4 5.4 %fusion.87 = f32[6,4096]{1,0:T(8,128)S(1)} fusion(s32[1024]{0:T(1024)S(1)} %bitcast.98, f32[6,4096]{1,0:T(8,128)S(1)} %get-tuple-element.372, pred[]{:T(512)S(6)} %compare.7, f32[16,6,1024]{2,1,0:T(8,128)S(1)} %get-tuple-element.379, s32[]{:T(128)} %get-tuple-element.371), kind=kOutput, calls=%fused_computation.27.clone.1 | convolution fusion | flops 306233344 | bytes 266245 | tf_op jit(solution)/shard_map/while/body/eval_jaxpr/dot_general | solution.py:67
  311.8 5.4 %fusion.87 = f32[6,4096]{1,0:T(8,128)S(1)} fusion(s32[1024]{0:T(1024)S(1)} %bitcast.98, f32[6,4096]{1,0:T(8,128)S(1)} %get-tuple-element.372, pred[]{:T(512)S(6)} %compare.7, f32[16,6,1024]{2,1,0:T(8,128)S(1)} %get-tuple-element.379, s32[]{:T(128)} %get-tuple-element.371), kind=kOutput, calls=%fused_computation.27.clone.1 | convolution fusion | flops 306233344 | bytes 266245 | tf_op jit(solution)/shard_map/while/body/eval_jaxpr/dot_general | solution.py:67
  317.2 5.4 %fusion.87 = f32[6,4096]{1,0:T(8,128)S(1)} fusion(s32[1024]{0:T(1024)S(1)} %bitcast.98, f32[6,4096]{1,0:T(8,128)S(1)} %get-tuple-element.372, pred[]{:T(512)S(6)} %compare.7, f32[16,6,1024]{2,1,0:T(8,128)S(1)} %get-tuple-element.379, s32[]{:T(128)} %get-tuple-element.371), kind=kOutput, calls=%fused_computation.27.clone.1 | convolution fusion | flops 306233344 | bytes 266245 | tf_op jit(solution)/shard_map/while/body/eval_jaxpr/dot_general | solution.py:67
  322.6 5.4 %fusion.87 = f32[6,4096]{1,0:T(8,128)S(1)} fusion(s32[1024]{0:T(1024)S(1)} %bitcast.98, f32[6,4096]{1,0:T(8,128)S(1)} %get-tuple-element.372, pred[]{:T(512)S(6)} %compare.7, f32[16,6,1024]{2,1,0:T(8,128)S(1)} %get-tuple-element.379, s32[]{:T(128)} %get-tuple-element.371), kind=kOutput, calls=%fused_computation.27.clone.1 | convolution fusion | flops 306233344 | bytes 266245 | tf_op jit(solution)/shard_map/while/body/eval_jaxpr/dot_general | solution.py:67
  (161 shorter events, 43.5 us)
Async XLA Ops:
  0.6 45.7 %copy-start = (f32[12,16]{1,0:T(8,128)S(1)}, f32[12,16]{1,0:T(8,128)}, u32[]{:S(2)}) copy-start(f32[12,16]{1,0:T(8,128)} %param.24) | copy-start | bytes 2308
  0.6 17.0 %copy-start.5 = (s32[128,128]{1,0:T(8,128)S(1)}, s32[128,128]{1,0:T(8,128)}, u32[]{:S(2)}) copy-start(s32[128,128]{1,0:T(8,128)} %param.28) | copy-start | bytes 196612
  1.7 8.3 %collective-permute-start = (f32[16,1,256]{2,1,0:T(1,128)S(1)}, f32[16,1,256]{2,1,0:T(1,128)S(1)}, u32[]{:S(2)}, u32[]{:S(2)}) collective-permute-start(f32[16,1,256]{2,1,0:T(1,128)S(1)} %get-tuple-element.216), channel_id=1, source_target_pairs={{32,0},{64,32},{96,64},{33,1},{65,33},{97,65},{34,2},{66,34},{98,6... | collective-permute-start | bytes 49160 | tf_op jit(solution)/shard_map/ppermute | solution.py:19
  3.0 7.0 %collective-permute-start.1 = (f32[16,1,256]{2,1,0:T(1,128)S(1)}, f32[16,1,256]{2,1,0:T(1,128)S(1)}, u32[]{:S(2)}, u32[]{:S(2)}) collective-permute-start(f32[16,1,256]{2,1,0:T(1,128)S(1)} %get-tuple-element.215), channel_id=1, source_target_pairs={{0,32},{32,64},{64,96},{1,33},{33,65},{65,97},{2,34},{34,66},{66,9... | collective-permute-start | bytes 49160 | tf_op jit(solution)/shard_map/ppermute | solution.py:16
  8.3 21.6 %copy-start.1 = (f32[16,16,256]{2,1,0:T(8,128)S(1)}, f32[16,16,256]{2,1,0:T(8,128)}, u32[]{:S(2)}) copy-start(f32[16,16,256]{2,1,0:T(8,128)} %param.21) | copy-start | bytes 786436
  8.3 21.6 %copy-start.4 = (f32[16,256]{1,0:T(8,128)S(1)}, f32[16,256]{1,0:T(8,128)}, u32[]{:S(2)}) copy-start(f32[16,256]{1,0:T(8,128)} %param.22) | copy-start | bytes 49156
  11.0 24.6 %copy-start.6 = (f32[128,128]{1,0:T(8,128)S(1)}, f32[128,128]{1,0:T(8,128)}, u32[]{:S(2)}) copy-start(f32[128,128]{1,0:T(8,128)} %param.29) | copy-start | bytes 196612
  11.0 24.6 %copy-start.13 = (s32[128]{0:T(128)S(1)}, s32[128]{0:T(128)}, u32[]{:S(2)}) copy-start(s32[128]{0:T(128)} %param.26) | copy-start | bytes 1540
  11.2 18.7 %collective-permute-start.2 = (f32[16,18,1]{2,1,0:T(8,128)S(1)}, f32[16,18,1]{2,1,0:T(8,128)S(1)}, u32[]{:S(2)}, u32[]{:S(2)}) collective-permute-start(f32[16,18,1]{2,1,0:T(8,128)S(1)} %get-tuple-element.211), channel_id=1, source_target_pairs={{1,0},{2,1},{3,2},{4,3},{5,4},{6,5},{7,6},{8,7},{9,8},{10,9},{11,1... | collective-permute-start | bytes 3464 | tf_op jit(solution)/shard_map/ppermute | solution.py:19
  14.5 15.4 %collective-permute-start.3 = (f32[16,18,1]{2,1,0:T(8,128)S(1)}, f32[16,18,1]{2,1,0:T(8,128)S(1)}, u32[]{:S(2)}, u32[]{:S(2)}) collective-permute-start(f32[16,18,1]{2,1,0:T(8,128)S(1)} %get-tuple-element.212), channel_id=1, source_target_pairs={{0,1},{1,2},{2,3},{3,4},{4,5},{5,6},{6,7},{7,8},{8,9},{9,10},{10,1... | collective-permute-start | bytes 3464 | tf_op jit(solution)/shard_map/ppermute | solution.py:16
  18.7 113.9 %all-to-all-start.1 = ((s32[1,128,256]{2,0,1:T(1,128)}), s32[1,128,256]{2,0,1:T(1,128)S(1)}, u32[]{:S(2)}, u32[]{:S(2)}) async-start(s32[1,128,256]{2,0,1:T(1,128)} %bitcast.8), calls=%async_computation.1 | async-start | bytes 262144 | tf_op jit(solution)/shard_map/all_to_all | solution.py:151
  30.3 13.0 %copy-start.9 = (s32[16,256]{1,0:T(8,128)S(1)}, s32[16,256]{1,0:T(8,128)}, u32[]{:S(2)}) copy-start(s32[16,256]{1,0:T(8,128)} %param.23) | copy-start | bytes 49156
  30.3 13.0 %copy-start.7 = (s32[128,128]{1,0:T(8,128)S(1)}, s32[128,128]{1,0:T(8,128)}, u32[]{:S(2)}) copy-start(s32[128,128]{1,0:T(8,128)} %param.27) | copy-start | bytes 196612
  30.3 5.4 %collective-permute-start.4 = (f32[16,1,256]{2,1,0:T(1,128)S(1)}, f32[16,1,256]{2,1,0:T(1,128)S(1)}, u32[]{:S(2)}, u32[]{:S(2)}) collective-permute-start(f32[16,1,256]{2,1,0:T(1,128)S(1)} %get-tuple-element.214), channel_id=1, source_target_pairs={{32,0},{64,32},{96,64},{33,1},{65,33},{97,65},{34,2},{66,34},{98,6... | collective-permute-start | bytes 49160 | tf_op jit(solution)/shard_map/ppermute | solution.py:19
  31.6 4.8 %collective-permute-start.5 = (f32[16,1,256]{2,1,0:T(1,128)S(1)}, f32[16,1,256]{2,1,0:T(1,128)S(1)}, u32[]{:S(2)}, u32[]{:S(2)}) collective-permute-start(f32[16,1,256]{2,1,0:T(1,128)S(1)} %get-tuple-element.213), channel_id=1, source_target_pairs={{0,32},{32,64},{64,96},{1,33},{33,65},{65,97},{2,34},{34,66},{66,9... | collective-permute-start | bytes 49160 | tf_op jit(solution)/shard_map/ppermute | solution.py:16
  36.6 8.0 %collective-permute-start.6 = (f32[16,18,1]{2,1,0:T(8,128)S(1)}, f32[16,18,1]{2,1,0:T(8,128)S(1)}, u32[]{:S(2)}, u32[]{:S(2)}) collective-permute-start(f32[16,18,1]{2,1,0:T(8,128)S(1)} %get-tuple-element.209), channel_id=1, source_target_pairs={{1,0},{2,1},{3,2},{4,3},{5,4},{6,5},{7,6},{8,7},{9,8},{10,9},{11,1... | collective-permute-start | bytes 3464 | tf_op jit(solution)/shard_map/ppermute | solution.py:19
  40.8 5.1 %collective-permute-start.7 = (f32[16,18,1]{2,1,0:T(8,128)S(1)}, f32[16,18,1]{2,1,0:T(8,128)S(1)}, u32[]{:S(2)}, u32[]{:S(2)}) collective-permute-start(f32[16,18,1]{2,1,0:T(8,128)S(1)} %get-tuple-element.210), channel_id=1, source_target_pairs={{0,1},{1,2},{2,3},{3,4},{4,5},{5,6},{6,7},{7,8},{8,9},{9,10},{10,1... | collective-permute-start | bytes 3464 | tf_op jit(solution)/shard_map/ppermute | solution.py:16
  46.2 0.7 copy-start.2
  132.6 12.2 %copy-start.11 = (s32[1024]{0:T(1024)S(1)}, s32[1024]{0:T(1024)}, u32[]{:S(2)}) copy-start(s32[1024]{0:T(1024)} %param.31) | copy-start | bytes 12292
  132.6 31.3 %all-to-all-start = ((bf16[12,128,256]{2,0,1:T(8,128)(2,1)}), bf16[12,128,256]{2,0,1:T(8,128)(2,1)S(1)}, u32[]{:S(2)}, u32[]{:S(2)}) async-start(bf16[12,128,256]{2,0,1:T(8,128)(2,1)} %copy.25), calls=%async_computation | async-start | bytes 2097152 | tf_op jit(solution)/shard_map/all_to_all | solution.py:144
  164.9 25.4 %copy-start.8 = (f32[8,1024]{1,0:T(8,128)S(1)}, f32[8,1024]{1,0:T(8,128)}, u32[]{:S(2)}) copy-start(f32[8,1024]{1,0:T(8,128)} %param.30) | copy-start | bytes 98308
  165.0 25.4 %copy-start.10 = (f32[8,12]{1,0:T(8,128)S(1)}, f32[8,12]{1,0:T(8,128)}, u32[]{:S(2)}) copy-start(f32[8,12]{1,0:T(8,128)} %param.32) | copy-start | bytes 1156
  165.0 25.5 %copy-start.12 = (f32[6,8]{1,0:T(8,128)S(1)}, f32[6,8]{1,0:T(8,128)}, u32[]{:S(2)}) copy-start(f32[6,8]{1,0:T(8,128)} %param.33) | copy-start | bytes 580
  190.5 0.6 copy-start.3
  222.7 18.2 %all-to-all-start.2 = ((bf16[6,128,256]{2,0,1:T(8,128)(2,1)}), bf16[6,128,256]{2,0,1:T(8,128)(2,1)S(1)}, u32[]{:S(2)}, u32[]{:S(2)}) async-start(bf16[6,128,256]{2,0,1:T(8,128)(2,1)} %bitcast.13), calls=%async_computation.2 | async-start | bytes 1048576 | tf_op jit(solution)/shard_map/all_to_all | solution.py:165
where the time goes:
time: 329 us
  matrix products  227 us (69%)
  starting transfers between devices  52.3 us (16%)
  waiting for transfers between devices  35.5 us (11%)
  local copies, waits for them, and re-layouts  7.32 us (2%)
  other arithmetic  4.54 us (1%)
    dot_general x16, matrix products, add_one_group(): jnp.dot(block_vals, one_hot, precision=lax.Precision.HIGHEST, preferred_e...  85.9 us
    dot_general x16, matrix products, pick_one_group(): jnp.dot(source_table, one_hot, precision=lax.Precision.HIGHEST, preferred...  82.7 us
    dot_general x16, matrix products, pick_one_group(): return jnp.dot(source_table, one_hot, preferred_element_type=jnp.float32)  31.3 us
    dot_general x16, matrix products, add_one_group(): added = jnp.dot(block_vals, one_hot, preferred_element_type=jnp.float32)  24.9 us
    all_to_all x1, waiting for transfers between devices, on_device(): lax.all_to_all(send_vals.reshape(flux_count, -1), ('grp', 'tile'), split_...  18.7 us
    ppermute x4, starting transfers between devices, with_halo(): lax.ppermute(lax.slice_in_dim(block, block.shape[dim] - width, None, axis...  14.2 us
    all_to_all x1, waiting for transfers between devices, on_device(): lax.all_to_all(picked, ('grp', 'tile'), split_axis=1, concat_axis=1, tile...  13.5 us
    all_to_all x1, starting transfers between devices, on_device(): lax.all_to_all(send_vals.reshape(flux_count, -1), ('grp', 'tile'), split_...  12.2 us
  transfers between devices with their start and end apart: 11, of which 5 were waited for; matrix products, arithmetic and copies ran while one was open for 28% of the time, Pallas kernels for 0%

commit v1 on v0

v1 whole, which is shorter than its diff:
```python
import functools

import jax
import jax.numpy as jnp
from jax import lax
from jax.experimental import pallas as pl
from jax.experimental.pallas import tpu as pltpu
from jax.sharding import PartitionSpec as P

MESH = pl.DeviceIdType.MESH
F32, BF16, I32 = jnp.float32, jnp.bfloat16, jnp.int32
NT = (((1,), (1,)), ((), ()))
G = 8


def iota(shape, dim):
    return lax.broadcasted_iota(I32, shape, dim)


def rows_of(row, count):
    return jnp.broadcast_to(row, (count, row.shape[1]))


def remote(src, dst, send_sem, recv_sem, device):
    return pltpu.make_async_remote_copy(
        src_ref=src,
        dst_ref=dst,
        send_sem=send_sem,
        recv_sem=recv_sem,
        device_id=device,
        device_id_type=MESH,
    )


def kernel(
    grps,
    tiles,
    atmos,
    kappa,
    sea_atm,
    flux_w,
    owner,
    count,
    source,
    dest,
    margin,
    ocean,
    sea_oc,
    couple,
    surf_w,
    atmos_out,
    ocean_out,
    atm_surf,
    mid,
    row_send,
    row_recv,
    col_send,
    col_recv,
    src_hi,
    src_lo,
    dst_hi,
    dst_lo,
    weight,
    hot_src,
    hot_dst,
    table32,
    table,
    fwd_send,
    fwd_recv,
    spread,
    surf32,
    back_send,
    back_recv,
    spread2,
    total,
    summed,
    halo_ss,
    halo_rs,
    fwd_ss,
    fwd_rs,
    back_ss,
    back_rs,
):
    devices = grps * tiles
    groups = devices // G
    width = G * 256
    g, t = lax.axis_index("grp"), lax.axis_index("tile")
    me = g * tiles + t

    def at(place):
        place = lax.rem(place, devices)
        return (place // tiles, lax.rem(place, tiles))

    barrier = pltpu.get_barrier_semaphore()

    @pl.loop(1, devices)
    def _(k):
        pl.semaphore_signal(barrier, inc=1, device_id=at(me + k), device_id_type=MESH)

    blocks = owner.shape[1]
    own_row = owner[...]
    own_here = jnp.broadcast_to(own_row, (blocks, blocks)).astype(F32)
    own_col = jnp.transpose(own_here)
    cnt_col = jnp.transpose(jnp.broadcast_to(count[...], (blocks, blocks)).astype(F32))
    before = iota((blocks, blocks), 0) < iota((blocks, blocks), 1)
    same = jnp.where((own_here == own_col) & before, F32(1), F32(0))
    rank = jnp.sum(same, axis=0, keepdims=True).astype(I32)
    ahead = own_row - me
    ahead = jnp.where(ahead < 0, ahead + devices, ahead)
    slot = ahead * 2 + rank
    place = jnp.where(
        iota((2 * devices, blocks), 0) == jnp.broadcast_to(slot, (2 * devices, blocks)), F32(1), F32(0)
    ).astype(BF16)

    def placed(values):
        return jnp.dot(place, values.astype(BF16), preferred_element_type=F32)

    src = source[...]
    src_hi[...] = placed((src >> 8).astype(F32))
    src_lo[...] = placed((src & 255).astype(F32))
    dst = dest[...]
    dst_hi[...] = placed((dst >> 7).astype(F32))
    dst_lo[...] = placed((dst & 127).astype(F32))
    lanes = iota((blocks, 128), 1).astype(F32)
    live = jnp.where(lanes < cnt_col[:, :1], margin[...], F32(0))
    first = live.astype(BF16).astype(F32)
    rest = live - first
    second = rest.astype(BF16).astype(F32)
    third = rest - second
    weight[...] = placed(first) + placed(second) + placed(third)

    ids16 = (iota((16, 16, 128), 0) * 16 + iota((16, 16, 128), 1)).astype(F32).astype(BF16)
    ids8 = (iota((8, 16, 128), 0) * 16 + iota((8, 16, 128), 1)).astype(F32).astype(BF16)
    one, zero = jnp.ones((16, 128), BF16), jnp.zeros((16, 128), BF16)

    @pl.loop(0, devices // 4)
    def _(i):
        low = src_lo[pl.ds(pl.multiple_of(i * 8, 8), 8), :]
        for j in range(8):
            lo = rows_of(low[j : j + 1], 16).astype(BF16)
            hot = jnp.where(ids16 == lo[None], one[None], zero[None])
            hot_src[:, pl.ds(pl.multiple_of(i * 1024 + j * 128, 128), 128)] = hot.reshape(256, 128)

    pl.semaphore_wait(barrier, devices - 1)

    rows, cols = atmos.shape[1], atmos.shape[2]
    chans = atmos.shape[0]
    row_id, col_id = iota((rows, cols), 0), iota((rows, cols), 1)
    lane = iota((rows, 128), 1)
    beside = (
        (lax.rem(g + grps - 1, grps), t),
        (lax.rem(g + 1, grps), t),
        (g, lax.rem(t + tiles - 1, tiles)),
        (g, lax.rem(t + 1, tiles)),
    )
    edge = (g == 0, g == grps - 1, t == 0, t == tiles - 1)
    diffusion = kappa[...]
    for step in range(2):
        state = atmos if step == 0 else mid
        west = jnp.zeros((rows, 128), F32)
        east = jnp.zeros((rows, 128), F32)
        for ch in range(chans):
            x = state[ch]
            row_send[step, 0, ch : ch + 1, :] = x[0:1]
            row_send[step, 1, ch : ch + 1, :] = x[rows - 1 : rows]
            west = jnp.where(lane == ch, x[:, 0:1], west)
            east = jnp.where(lane == ch, x[:, cols - 1 : cols], east)
        col_send[step, 0] = west
        col_send[step, 1] = east
        copies = []
        for side in range(4):
            sent, got = (row_send, row_recv) if side < 2 else (col_send, col_recv)
            copies.append(
                remote(
                    sent.at[step, side % 2],
                    got.at[step, 1 - side % 2],
                    halo_ss.at[step, side],
                    halo_rs.at[step, side],
                    beside[side],
                )
            )
        for copy in copies:
            copy.start()
        for copy in copies:
            copy.wait()
        north = jnp.where(edge[0], F32(0), row_recv[step, 0])
        south = jnp.where(edge[1], F32(0), row_recv[step, 1])
        west = jnp.where(edge[2], F32(0), col_recv[step, 0])
        east = jnp.where(edge[3], F32(0), col_recv[step, 1])
        for ch in range(chans):
            x = state[ch]
            up = jnp.where(row_id == 0, north[ch : ch + 1], pltpu.roll(x, 1, 0))
            down = jnp.where(row_id == rows - 1, south[ch : ch + 1], pltpu.roll(x, rows - 1, 0))
            left = jnp.where(col_id == 0, west[:, ch : ch + 1], pltpu.roll(x, 1, 1))
            right = jnp.where(col_id == cols - 1, east[:, ch : ch + 1], pltpu.roll(x, cols - 1, 1))
            new = x + diffusion * (down + up + right + left - 4.0 * x)
            if step == 0:
                mid[ch] = new
            else:
                atmos_out[ch] = new

    sea = sea_atm[...] > 0
    for f in range(12):
        mixed = flux_w[f, 0] * atmos_out[0]
        for ch in range(1, chans):
            mixed = mixed + flux_w[f, ch] * atmos_out[ch]
        flux = jnp.where(sea, jnp.tanh(mixed), F32(0))
        for half in range(2):
            part = flux[:, half * 128 : half * 128 + 128]
            if f < 8:
                table32[half, pl.ds(f, 16, stride=8), :] = part
            else:
                table32[half, pl.ds(128 + f - 8, 16, stride=4), :] = part
    for half in range(2):
        full = table32[half]
        top = full.astype(BF16)
        table[:, half * 128 : half * 128 + 128] = top
        table[:, 256 + half * 128 : 384 + half * 128] = (full - top.astype(F32)).astype(BF16)

    sub = iota((8, 128), 0)
    odd = jnp.where(sub >= 4, F32(1), F32(0))

    @pl.loop(0, groups)
    def _(i):
        hot = hot_src[:, pl.ds(pl.multiple_of(i * width, width), width)]
        found = jnp.dot(table[...], jnp.concatenate([hot, hot], axis=0), preferred_element_type=F32)
        here = pl.ds(pl.multiple_of(i * 2 * G, 2 * G), 2 * G)
        hi, w, dh, dl = src_hi[here, :], weight[here, :], dst_hi[here, :], dst_lo[here, :]
        for j in range(2 * G):
            mine = found[:, j * 128 : j * 128 + 128]
            h = rows_of(hi[j : j + 1], 8)
            wide = mine[0:8]
            for v in range(1, 16):
                wide = jnp.where(h == v, mine[v * 8 : v * 8 + 8], wide)
            h = h - odd
            thin = jnp.zeros((8, 128), F32)
            for v in range(8):
                thin = jnp.where(h == 2 * v, mine[128 + v * 8 : 136 + v * 8], thin)
            thin = thin + pltpu.roll(thin, 4, 0)
            scale = rows_of(w[j : j + 1], 8)
            thin = jnp.where(sub == 4, rows_of(dh[j : j + 1], 8), thin * scale)
            thin = jnp.where(sub == 5, rows_of(dl[j : j + 1], 8), thin)
            fwd_send[i * G + j // 2, j % 2] = jnp.concatenate([wide * scale, thin], axis=0).astype(BF16)
        for j in range(G):
            k = i * G + j

            @pl.when(k > 0)
            def _():
                remote(
                    fwd_send.at[k], fwd_recv.at[k], fwd_ss.at[k], fwd_rs.at[k], at(me + k)
                ).start()

    fwd_recv[0] = fwd_send[0]

    total[...] = jnp.zeros_like(total)

    @pl.loop(0, groups)
    def _(i):
        for j in range(G):
            k = i * G + j

            @pl.when(k > 0)
            def _():
                remote(
                    fwd_send.at[k], fwd_recv.at[k], fwd_ss.at[k], fwd_rs.at[k], at(me + k)
                ).wait_recv()

        for j in range(2 * G):
            tile = fwd_recv[i * G + j // 2, j % 2]
            wide = tile.astype(F32)
            hi = rows_of(wide[12:13], 16).astype(BF16)
            lo = rows_of(wide[13:14], 16).astype(BF16)
            for v in range(8):
                spread[v * 16 : v * 16 + 16, j * 128 : j * 128 + 128] = jnp.where(hi == v, tile, zero)
            hot = jnp.where(ids8 == lo[None], one[None], zero[None])
            hot_dst[:, pl.ds(pl.multiple_of(i * width + j * 128, 128), 128)] = hot.reshape(128, 128)
        total[...] += lax.dot_general(
            spread[...],
            hot_dst[:, pl.ds(pl.multiple_of(i * width, width), width)],
            NT,
            preferred_element_type=F32,
        )

    surf32[...] = jnp.zeros_like(surf32)
    for h in range(8):
        here = slice(h * 128, h * 128 + 128)
        flux = total[h * 16 : h * 16 + 16, :]
        added = couple[:, 0:1] * flux[0:1]
        for f in range(1, 12):
            added = added + couple[:, f : f + 1] * flux[f : f + 1]
        new = ocean[:, here] + jnp.where(sea_oc[:, here] > 0, added, F32(0))
        ocean_out[:, here] = new
        field = surf_w[:, 0:1] * new[0:1]
        for o in range(1, 8):
            field = field + surf_w[:, o : o + 1] * new[o : o + 1]
        surf32[h * 8 : h * 8 + 6, :] = jnp.tanh(field)
    surface = surf32[...].astype(BF16)

    @pl.loop(0, groups)
    def _(i):
        found = jnp.dot(
            surface,
            hot_dst[:, pl.ds(pl.multiple_of(i * width, width), width)],
            preferred_element_type=F32,
        )
        for j in range(G):
            k = i * G + j
            both = []
            for part in range(2):
                mine = found[:, (2 * j + part) * 128 : (2 * j + part) * 128 + 128]
                tile = fwd_recv[k, part].astype(F32)
                h = rows_of(tile[12:13], 8)
                got = mine[0:8]
                for v in range(1, 8):
                    got = jnp.where(h == v, mine[v * 8 : v * 8 + 8], got)
                both.append(got)
            back_send[k] = jnp.concatenate(both, axis=0).astype(BF16)
        for j in range(G):
            k = i * G + j

            @pl.when(k > 0)
            def _():
                remote(
                    back_send.at[k], back_recv.at[k], back_ss.at[k], back_rs.at[k], at(me + devices - k)
                ).start()

    back_recv[0] = back_send[0]

    summed[...] = jnp.zeros_like(summed)

    @pl.loop(0, groups)
    def _(i):
        for j in range(G):
            k = i * G + j

            @pl.when(k > 0)
            def _():
                remote(
                    back_send.at[k], back_recv.at[k], back_ss.at[k], back_rs.at[k], at(me + devices - k)
                ).wait_recv()

        here = pl.ds(pl.multiple_of(i * 2 * G, 2 * G), 2 * G)
        hi, w = src_hi[here, :], weight[here, :]
        for j in range(2 * G):
            both = back_recv[i * G + j // 2].astype(F32)
            value = both[(j % 2) * 8 : (j % 2) * 8 + 8] * rows_of(w[j : j + 1], 8)
            top = value.astype(BF16).astype(F32)
            pair = jnp.concatenate([top, value - top], axis=0).astype(BF16)
            h = rows_of(hi[j : j + 1], 16).astype(BF16)
            for v in range(16):
                spread2[v * 16 : v * 16 + 16, j * 128 : j * 128 + 128] = jnp.where(h == v, pair, zero)
        summed[...] += lax.dot_general(
            spread2[...],
            hot_src[:, pl.ds(pl.multiple_of(i * width, width), width)],
            NT,
            preferred_element_type=F32,
        )

    for half in range(2):
        here = slice(half * 128, half * 128 + 128)
        for h in range(16):
            table32[half, h * 8 : h * 8 + 8, :] = (
                summed[h * 16 : h * 16 + 8, here] + summed[h * 16 + 8 : h * 16 + 16, here]
            )
        for s in range(6):
            atm_surf[s, :, here] = jnp.where(
                sea[:, here], table32[half, pl.ds(s, 16, stride=8), :], F32(0)
            )

    @pl.loop(1, devices)
    def _(k):
        remote(fwd_send.at[k], fwd_recv.at[k], fwd_ss.at[k], fwd_rs.at[k], at(me + k)).wait_send()
        remote(
            back_send.at[k], back_recv.at[k], back_ss.at[k], back_rs.at[k], at(me + devices - k)
        ).wait_send()


def on_device(grps, tiles, *args):
    (
        atmos,
        diffusivity,
        sea_atm,
        flux_weight,
        block_owner,
        entry_count,
        source_col,
        dest_col,
        margin,
        ocean,
        sea_ocean,
        couple,
        surface_weight,
    ) = args
    devices = grps * tiles
    slots = 2 * devices
    vmem = pl.BlockSpec(memory_space=pltpu.VMEM)
    smem = pl.BlockSpec(memory_space=pltpu.SMEM)
    chans, rows, cols = atmos.shape
    dma = pltpu.SemaphoreType.DMA
    return pl.pallas_call(
        functools.partial(kernel, grps, tiles),
        out_shape=(
            jax.ShapeDtypeStruct(atmos.shape, F32),
            jax.ShapeDtypeStruct(ocean.shape, F32),
            jax.ShapeDtypeStruct((6, rows, cols), F32),
        ),
        in_specs=[vmem, vmem, vmem, smem] + [vmem] * 9,
        out_specs=(vmem, vmem, vmem),
        scratch_shapes=[
            pltpu.VMEM((chans, rows, cols), F32),
            pltpu.VMEM((2, 2, chans, cols), F32),
            pltpu.VMEM((2, 2, chans, cols), F32),
            pltpu.VMEM((2, 2, rows, 128), F32),
            pltpu.VMEM((2, 2, rows, 128), F32),
            pltpu.VMEM((slots, 128), F32),
            pltpu.VMEM((slots, 128), F32),
            pltpu.VMEM((slots, 128), F32),
            pltpu.VMEM((slots, 128), F32),
            pltpu.VMEM((slots, 128), F32),
            pltpu.VMEM((256, slots * 128), BF16),
            pltpu.VMEM((128, slots * 128), BF16),
            pltpu.VMEM((2, 192, 128), F32),
            pltpu.VMEM((192, 512), BF16),
            pltpu.VMEM((devices, 2, 16, 128), BF16),
            pltpu.VMEM((devices, 2, 16, 128), BF16),
            pltpu.VMEM((128, G * 256), BF16),
            pltpu.VMEM((64, 128), F32),
            pltpu.VMEM((devices, 16, 128), BF16),
            pltpu.VMEM((devices, 16, 128), BF16),
            pltpu.VMEM((256, G * 256), BF16),
            pltpu.VMEM((128, 128), F32),
            pltpu.VMEM((256, 256), F32),
            dma((2, 4)),
            dma((2, 4)),
            dma((devices,)),
            dma((devices,)),
            dma((devices,)),
            dma((devices,)),
        ],
        compiler_params=pltpu.CompilerParams(
            collective_id=0, has_side_effects=True, vmem_limit_bytes=56 * 1024 * 1024
        ),
    )(
        atmos,
        diffusivity,
        sea_atm,
        flux_weight,
        block_owner.reshape(1, -1),
        entry_count.reshape(1, -1),
        source_col,
        dest_col,
        margin,
        ocean,
        sea_ocean.reshape(1, -1),
        couple,
        surface_weight,
    )


def solution(mesh):
    placed = (
        P(None, "grp", "tile"),
        P("grp", "tile"),
        P("grp", "tile"),
        P(),
        P(("grp", "tile"), None),
        P(("grp", "tile")),
        P(("grp", "tile"), None),
        P(("grp", "tile"), None),
        P(("grp", "tile"), None),
        P(None, ("grp", "tile")),
        P(("grp", "tile")),
        P(),
        P(),
    )
    return jax.shard_map(
        functools.partial(on_device, mesh.shape["grp"], mesh.shape["tile"]),
        mesh=mesh,
        in_specs=placed,
        out_specs=(P(None, "grp", "tile"), P(None, ("grp", "tile")), P(None, "grp", "tile")),
        check_vma=False,
    )
```

time: 329 us -> 69.7 us (0.21)
  matrix products: 227 us -> 0 us
  Pallas kernels: 0 us -> 65.3 us
  starting transfers between devices: 52.3 us -> 0 us
  waiting for transfers between devices: 35.5 us -> 0 us
  other arithmetic: 4.54 us -> 0 us
  local copies, waits for them, and re-layouts: 7.32 us -> 2.97 us
    dot_general x70 -> x0, matrix products: 227 us -> none  [the longest x16 85.9 us: add_one_group(): jnp.dot(block_vals, one_hot, precision=lax.Precision.HIGHEST, preferred_e...]
    pallas_call x0 -> x1, Pallas kernels: none -> 65.3 us  [on_device(): pl.pallas_call(functools.partial(kernel, grps, tiles), out_shape=(jax.Sha...]
    all_to_all x3 -> x0, waiting for transfers between devices: 32.2 us -> none  [the longest x1 18.7 us: on_device(): lax.all_to_all(send_vals.reshape(flux_count, -1), ('grp', 'tile'), split_...]
    all_to_all x3 -> x0, starting transfers between devices: 28.1 us -> none  [the longest x1 12.2 us: on_device(): lax.all_to_all(send_vals.reshape(flux_count, -1), ('grp', 'tile'), split_...]
    ppermute x8 -> x0, starting transfers between devices: 24.2 us -> none  [the longest x4 14.2 us: with_halo(): lax.ppermute(lax.slice_in_dim(block, block.shape[dim] - width, None, axis...]
  transfers between devices with their start and end apart: 11 -> 0, of which waited for: 5 -> 0; matrix products, arithmetic and copies ran while one was open for 28% -> 0% of each run, Pallas kernels for 0% -> 0%
where the time goes in v1:
time: 69.7 us; the launch traced here: 68.9 us
  Pallas kernels  65.3 us (94%)
  local copies, waits for them, and re-layouts  2.97 us (4%)
    pallas_call x1, Pallas kernels, on_device(): pl.pallas_call(functools.partial(kernel, grps, tiles), out_shape=(jax.Sha...  65.3 us
    unnamed x7, local copies, waits for them, and re-layouts  2.97 us

profile of v1, /device:TPU:1, one launch (start us, length us, event | category | flops | bytes accessed | tf_op | source)
XLA Modules:
  0.0 68.9 jit_solution(16834623964567787007)
XLA Ops:
  0.6 65.3 %shard_map.148 = (f32[16,16,256]{2,1,0:T(8,128)}, f32[8,1024]{1,0:T(8,128)}, f32[6,16,256]{2,1,0:T(8,128)}) custom-call(f32[16,16,256]{2,1,0:T(8,128)} %atmos.1, f32[16,256]{1,0:T(8,128)} %kappa.1, s32[16,256]{1,0:T(8,128)} %sea_atm.1, f32[12,16]{1,0:T(8,128)} %flux_w.1, s32[1,128]{1,0:T(1,128)} %bitcast.4, s32[1,128]{1,0:T(1,128)} %bitcast.5, ...), custom_call_target="tpu_custom_call" | custom-call | tf_op jit(solution)/shard_map/pallas_call | solution.py:400
  65.9 0.0 copy-start.1
  65.9 0.0 copy-start
  65.9 1.7 %copy.19 = f32[16,16,256]{2,1,0:T(8,128)} copy(f32[16,16,256]{2,1,0:T(8,128)} %get-tuple-element.6) | data formatting | bytes 524288
  67.6 0.0 copy-done.1
  67.6 0.6 copy.20
  68.3 0.0 copy-done
  68.3 0.6 copy.21
Async XLA Ops:
  65.9 1.7 %copy-start.1 = (f32[8,1024]{1,0:T(8,128)S(1)}, f32[8,1024]{1,0:T(8,128)}, u32[]{:S(2)}) copy-start(f32[8,1024]{1,0:T(8,128)} %get-tuple-element.7) | copy-start | bytes 98308
  65.9 2.3 %copy-start = (f32[6,16,256]{2,1,0:T(8,128)S(1)}, f32[6,16,256]{2,1,0:T(8,128)}, u32[]{:S(2)}) copy-start(f32[6,16,256]{2,1,0:T(8,128)} %get-tuple-element.8) | copy-start | bytes 294916

commit v2 on v1

--- a/solution.py
+++ b/solution.py
@@ -35,19 +35,29 @@
 def kernel(
     grps,
     tiles,
+    atmos_in,
+    kappa_in,
+    sea_atm_in,
+    flux_w,
+    owner,
+    count,
+    source_in,
+    dest_in,
+    margin_in,
+    ocean_in,
+    sea_oc,
+    couple,
+    surf_w,
+    atmos_to,
+    ocean_to,
+    surf_to,
     atmos,
     kappa,
     sea_atm,
-    flux_w,
-    owner,
-    count,
     source,
     dest,
     margin,
     ocean,
-    sea_oc,
-    couple,
-    surf_w,
     atmos_out,
     ocean_out,
     atm_surf,
@@ -58,8 +68,10 @@
     col_recv,
     src_hi,
     src_lo,
+    dst_all,
+    dst_send,
+    dst_recv,
     dst_hi,
-    dst_lo,
     weight,
     hot_src,
     hot_dst,
@@ -76,10 +88,14 @@
     summed,
     halo_ss,
     halo_rs,
+    dst_ss,
+    dst_rs,
     fwd_ss,
     fwd_rs,
     back_ss,
     back_rs,
+    in_sem,
+    out_sem,
 ):
     devices = grps * tiles
     groups = devices // G
@@ -87,15 +103,76 @@
     g, t = lax.axis_index("grp"), lax.axis_index("tile")
     me = g * tiles + t
 
-    def at(place):
-        place = lax.rem(place, devices)
-        return (place // tiles, lax.rem(place, tiles))
+    z, y, core = t // 8, lax.rem(t // 2, 4), lax.rem(t, 2)
+
+    def peer(i, j, back=False):
+        s, c = j // 2, j % 2
+        dz, dy = i // 4 + s, lax.rem(i, 4) + s
+        if back:
+            s, dz, dy = 4 - s, 8 - dz, 8 - dy
+        row = lax.rem(z + dz, 4) * 8 + lax.rem(y + dy, 4) * 2 + lax.rem(core + c, 2)
+        return (lax.rem(g + s, 4), row)
+
+    def dest_copy(i, j):
+        k = i * G + j
+        return remote(dst_send.at[k], dst_recv.at[k], dst_ss, dst_rs, peer(i, j))
+
+    def fwd_copy(i, j):
+        k = i * G + j
+        return remote(fwd_send.at[k], fwd_recv.at[k], fwd_ss, fwd_rs.at[i], peer(i, j))
+
+    def back_copy(i, j):
+        k = i * G + j
+        return remote(back_send.at[k], back_recv.at[k], back_ss, back_rs.at[i], peer(i, j, True))
+
+    def others(i, act):
+        for j in range(G):
+            if j == 0:
+
+                @pl.when(i > 0)
+                def _():
+                    act(i, 0)
+            else:
+                act(i, j)
+
+    def settle(buffer, sem, start, size):
+        part = buffer.at[pl.ds(start, size)]
+        pltpu.make_async_copy(part, part, sem).wait()
+
+    def settle_group(buffer, sems, i):
+        @pl.when(i == 0)
+        def _():
+            settle(buffer, sems.at[0], 1, G - 1)
+
+        @pl.when(i > 0)
+        def _():
+            settle(buffer, sems.at[i], i * G, G)
 
     barrier = pltpu.get_barrier_semaphore()
 
-    @pl.loop(1, devices)
-    def _(k):
-        pl.semaphore_signal(barrier, inc=1, device_id=at(me + k), device_id_type=MESH)
+    @pl.loop(0, groups)
+    def _(i):
+        others(
+            i,
+            lambda i, j: pl.semaphore_signal(
+                barrier, inc=1, device_id=peer(i, j), device_id_type=MESH
+            ),
+        )
+
+    loads = {}
+    for n, (name, a, b) in enumerate(
+        (
+            ("source", source_in, source),
+            ("dest", dest_in, dest),
+            ("margin", margin_in, margin),
+            ("atmos", atmos_in, atmos),
+            ("kappa", kappa_in, kappa),
+            ("sea", sea_atm_in, sea_atm),
+            ("ocean", ocean_in, ocean),
+        )
+    ):
+        loads[name] = pltpu.make_async_copy(a, b, in_sem.at[n])
+        loads[name].start()
 
     blocks = owner.shape[1]
     own_row = owner[...]
@@ -105,9 +182,11 @@
     before = iota((blocks, blocks), 0) < iota((blocks, blocks), 1)
     same = jnp.where((own_here == own_col) & before, F32(1), F32(0))
     rank = jnp.sum(same, axis=0, keepdims=True).astype(I32)
-    ahead = own_row - me
-    ahead = jnp.where(ahead < 0, ahead + devices, ahead)
-    slot = ahead * 2 + rank
+    dx = ((own_row >> 5) - g) & 3
+    dz = (((own_row >> 3) & 3) - z - dx) & 3
+    dy = (((own_row >> 1) & 3) - y - dx) & 3
+    dc = ((own_row & 1) - core) & 1
+    slot = (((dz * 4 + dy) * 4 + dx) * 2 + dc) * 2 + rank
     place = jnp.where(
         iota((2 * devices, blocks), 0) == jnp.broadcast_to(slot, (2 * devices, blocks)), F32(1), F32(0)
     ).astype(BF16)
@@ -115,12 +194,21 @@
     def placed(values):
         return jnp.dot(place, values.astype(BF16), preferred_element_type=F32)
 
+    for name in ("source", "dest", "margin"):
+        loads[name].wait()
     src = source[...]
     src_hi[...] = placed((src >> 8).astype(F32))
     src_lo[...] = placed((src & 255).astype(F32))
     dst = dest[...]
-    dst_hi[...] = placed((dst >> 7).astype(F32))
-    dst_lo[...] = placed((dst & 127).astype(F32))
+    dst_all[...] = placed((dst >> 7).astype(F32)) * 128.0 + placed((dst & 127).astype(F32))
+
+    @pl.loop(0, devices // 4)
+    def _(i):
+        four = dst_all[pl.ds(pl.multiple_of(i * 8, 8), 8), :]
+        for j in range(4):
+            dst_send[i * 4 + j] = four[2 * j : 2 * j + 2]
+
+    dst_recv[0] = dst_send[0]
     lanes = iota((blocks, 128), 1).astype(F32)
     live = jnp.where(lanes < cnt_col[:, :1], margin[...], F32(0))
     first = live.astype(BF16).astype(F32)
@@ -141,6 +229,8 @@
             hot = jnp.where(ids16 == lo[None], one[None], zero[None])
             hot_src[:, pl.ds(pl.multiple_of(i * 1024 + j * 128, 128), 128)] = hot.reshape(256, 128)
 
+    for name in ("atmos", "kappa", "sea", "ocean"):
+        loads[name].wait()
     pl.semaphore_wait(barrier, devices - 1)
 
     rows, cols = atmos.shape[1], atmos.shape[2]
@@ -181,6 +271,12 @@
             )
         for copy in copies:
             copy.start()
+        if step == 0:
+
+            @pl.loop(0, groups)
+            def _(i):
+                others(i, lambda i, j: dest_copy(i, j).start())
+
         for copy in copies:
             copy.wait()
         north = jnp.where(edge[0], F32(0), row_recv[step, 0])
@@ -199,6 +295,9 @@
             else:
                 atmos_out[ch] = new
 
+    stores = [pltpu.make_async_copy(atmos_out, atmos_to, out_sem.at[0])]
+    stores[0].start()
+
     sea = sea_atm[...] > 0
     for f in range(12):
         mixed = flux_w[f, 0] * atmos_out[0]
@@ -213,67 +312,70 @@
                 table32[half, pl.ds(128 + f - 8, 16, stride=4), :] = part
     for half in range(2):
         full = table32[half]
-        top = full.astype(BF16)
-        table[:, half * 128 : half * 128 + 128] = top
-        table[:, 256 + half * 128 : 384 + half * 128] = (full - top.astype(F32)).astype(BF16)
+        table[:, half * 128 : half * 128 + 128] = full.astype(BF16)
 
     sub = iota((8, 128), 0)
     odd = jnp.where(sub >= 4, F32(1), F32(0))
 
     @pl.loop(0, groups)
     def _(i):
-        hot = hot_src[:, pl.ds(pl.multiple_of(i * width, width), width)]
-        found = jnp.dot(table[...], jnp.concatenate([hot, hot], axis=0), preferred_element_type=F32)
         here = pl.ds(pl.multiple_of(i * 2 * G, 2 * G), 2 * G)
-        hi, w, dh, dl = src_hi[here, :], weight[here, :], dst_hi[here, :], dst_lo[here, :]
-        for j in range(2 * G):
-            mine = found[:, j * 128 : j * 128 + 128]
-            h = rows_of(hi[j : j + 1], 8)
-            wide = mine[0:8]
-            for v in range(1, 16):
-                wide = jnp.where(h == v, mine[v * 8 : v * 8 + 8], wide)
-            h = h - odd
-            thin = jnp.zeros((8, 128), F32)
-            for v in range(8):
-                thin = jnp.where(h == 2 * v, mine[128 + v * 8 : 136 + v * 8], thin)
-            thin = thin + pltpu.roll(thin, 4, 0)
-            scale = rows_of(w[j : j + 1], 8)
-            thin = jnp.where(sub == 4, rows_of(dh[j : j + 1], 8), thin * scale)
-            thin = jnp.where(sub == 5, rows_of(dl[j : j + 1], 8), thin)
-            fwd_send[i * G + j // 2, j % 2] = jnp.concatenate([wide * scale, thin], axis=0).astype(BF16)
+        hi, w = src_hi[here, :], weight[here, :]
         for j in range(G):
-            k = i * G + j
-
-            @pl.when(k > 0)
-            def _():
-                remote(
-                    fwd_send.at[k], fwd_recv.at[k], fwd_ss.at[k], fwd_rs.at[k], at(me + k)
-                ).start()
+            hot = hot_src[:, pl.ds(pl.multiple_of(i * width + j * 256, 256), 256)]
+            found = jnp.dot(table[...], hot, preferred_element_type=F32)
+            ends = []
+            for part in range(2):
+                mine = found[:, part * 128 : part * 128 + 128]
+                h = rows_of(hi[2 * j + part : 2 * j + part + 1], 8)
+                wide = mine[0:8]
+                for v in range(1, 16):
+                    wide = jnp.where(h == v, mine[v * 8 : v * 8 + 8], wide)
+                h = h - odd
+                thin = jnp.zeros((8, 128), F32)
+                for v in range(8):
+                    thin = jnp.where(h == 2 * v, mine[128 + v * 8 : 136 + v * 8], thin)
+                scale = rows_of(w[2 * j + part : 2 * j + part + 1], 8)
+                fwd_send[i * G + j, part] = (wide * scale).astype(BF16)
+                ends.append((thin + pltpu.roll(thin, 4, 0)) * scale)
+            fwd_send[i * G + j, 2] = jnp.where(sub < 4, ends[0], ends[1]).astype(BF16)
+        others(i, lambda i, j: fwd_copy(i, j).start())
 
     fwd_recv[0] = fwd_send[0]
 
+    settle(dst_recv, dst_rs, 1, devices - 1)
+
+    @pl.loop(0, groups)
+    def _(i):
+        for j in range(G):
+            where = dst_recv[i * G + j]
+            high = jnp.floor(where * (1 / 128))
+            dst_hi[i * G + j] = high
+            low = where - high * 128.0
+            for part in range(2):
+                lo = rows_of(low[part : part + 1], 16).astype(BF16)
+                hot = jnp.where(ids8 == lo[None], one[None], zero[None])
+                hot_dst[:, pl.ds(pl.multiple_of(i * width + j * 256 + part * 128, 128), 128)] = hot.reshape(
+                    128, 128
+                )
+
     total[...] = jnp.zeros_like(total)
 
     @pl.loop(0, groups)
     def _(i):
+        settle_group(fwd_recv, fwd_rs, i)
         for j in range(G):
-            k = i * G + j
-
-            @pl.when(k > 0)
-            def _():
-                remote(
-                    fwd_send.at[k], fwd_recv.at[k], fwd_ss.at[k], fwd_rs.at[k], at(me + k)
-                ).wait_recv()
-
-        for j in range(2 * G):
-            tile = fwd_recv[i * G + j // 2, j % 2]
-            wide = tile.astype(F32)
-            hi = rows_of(wide[12:13], 16).astype(BF16)
-            lo = rows_of(wide[13:14], 16).astype(BF16)
-            for v in range(8):
-                spread[v * 16 : v * 16 + 16, j * 128 : j * 128 + 128] = jnp.where(hi == v, tile, zero)
-            hot = jnp.where(ids8 == lo[None], one[None], zero[None])
-            hot_dst[:, pl.ds(pl.multiple_of(i * width + j * 128, 128), 128)] = hot.reshape(128, 128)
+            high = dst_hi[i * G + j]
+            ends = fwd_recv[i * G + j, 2].astype(F32)
+            for part in range(2):
+                tile = jnp.concatenate(
+                    [fwd_recv[i * G + j, part].astype(F32), pltpu.roll(ends, 4, 0) if part else ends],
+                    axis=0,
+                ).astype(BF16)
+                hi = rows_of(high[part : part + 1], 16).astype(BF16)
+                at = slice(j * 256 + part * 128, j * 256 + part * 128 + 128)
+                for v in range(8):
+                    spread[v * 16 : v * 16 + 16, at] = jnp.where(hi == v, tile, zero)
         total[...] += lax.dot_general(
             spread[...],
             hot_dst[:, pl.ds(pl.multiple_of(i * width, width), width)],
@@ -295,34 +397,31 @@
             field = field + surf_w[:, o : o + 1] * new[o : o + 1]
         surf32[h * 8 : h * 8 + 6, :] = jnp.tanh(field)
     surface = surf32[...].astype(BF16)
+    stores.append(pltpu.make_async_copy(ocean_out, ocean_to, out_sem.at[1]))
+    stores[1].start()
 
     @pl.loop(0, groups)
     def _(i):
-        found = jnp.dot(
-            surface,
-            hot_dst[:, pl.ds(pl.multiple_of(i * width, width), width)],
-            preferred_element_type=F32,
-        )
         for j in range(G):
             k = i * G + j
+            found = jnp.dot(
+                surface,
+                hot_dst[:, pl.ds(pl.multiple_of(i * width + j * 256, 256), 256)],
+                preferred_element_type=F32,
+            )
+            high = dst_hi[k]
             both = []
             for part in range(2):
-                mine = found[:, (2 * j + part) * 128 : (2 * j + part) * 128 + 128]
-                tile = fwd_recv[k, part].astype(F32)
-                h = rows_of(tile[12:13], 8)
+                mine = found[:, part * 128 : part * 128 + 128]
+                h = rows_of(high[part : part + 1], 8)
                 got = mine[0:8]
                 for v in range(1, 8):
                     got = jnp.where(h == v, mine[v * 8 : v * 8 + 8], got)
+                back_send[k, part] = got[0:4].astype(BF16)
                 both.append(got)
-            back_send[k] = jnp.concatenate(both, axis=0).astype(BF16)
-        for j in range(G):
-            k = i * G + j
-
-            @pl.when(k > 0)
-            def _():
-                remote(
-                    back_send.at[k], back_recv.at[k], back_ss.at[k], back_rs.at[k], at(me + devices - k)
-                ).start()
+            ends = jnp.where(sub < 2, pltpu.roll(both[0], 4, 0), pltpu.roll(both[1], 6, 0))
+            back_send[k, 2] = ends[0:4].astype(BF16)
+        others(i, lambda i, j: back_copy(i, j).start())
 
     back_recv[0] = back_send[0]
 
@@ -330,25 +429,22 @@
 
     @pl.loop(0, groups)
     def _(i):
-        for j in range(G):
-            k = i * G + j
-
-            @pl.when(k > 0)
-            def _():
-                remote(
-                    back_send.at[k], back_recv.at[k], back_ss.at[k], back_rs.at[k], at(me + devices - k)
-                ).wait_recv()
-
+        settle_group(back_recv, back_rs, i)
         here = pl.ds(pl.multiple_of(i * 2 * G, 2 * G), 2 * G)
         hi, w = src_hi[here, :], weight[here, :]
-        for j in range(2 * G):
-            both = back_recv[i * G + j // 2].astype(F32)
-            value = both[(j % 2) * 8 : (j % 2) * 8 + 8] * rows_of(w[j : j + 1], 8)
-            top = value.astype(BF16).astype(F32)
-            pair = jnp.concatenate([top, value - top], axis=0).astype(BF16)
-            h = rows_of(hi[j : j + 1], 16).astype(BF16)
-            for v in range(16):
-                spread2[v * 16 : v * 16 + 16, j * 128 : j * 128 + 128] = jnp.where(h == v, pair, zero)
+        for j in range(G):
+            ends = back_recv[i * G + j, 2].astype(F32)
+            for part in range(2):
+                most = back_recv[i * G + j, part].astype(F32)
+                last = [ends[2:4], ends[0:2]] if part else [ends]
+                value = jnp.concatenate([most] + last, axis=0)
+                value = value * rows_of(w[2 * j + part : 2 * j + part + 1], 8)
+                top = value.astype(BF16).astype(F32)
+                pair = jnp.concatenate([top, value - top], axis=0).astype(BF16)
+                h = rows_of(hi[2 * j + part : 2 * j + part + 1], 16).astype(BF16)
+                at = slice(j * 256 + part * 128, j * 256 + part * 128 + 128)
+                for v in range(16):
+                    spread2[v * 16 : v * 16 + 16, at] = jnp.where(h == v, pair, zero)
         summed[...] += lax.dot_general(
             spread2[...],
             hot_src[:, pl.ds(pl.multiple_of(i * width, width), width)],
@@ -367,12 +463,25 @@
                 sea[:, here], table32[half, pl.ds(s, 16, stride=8), :], F32(0)
             )
 
-    @pl.loop(1, devices)
-    def _(k):
-        remote(fwd_send.at[k], fwd_recv.at[k], fwd_ss.at[k], fwd_rs.at[k], at(me + k)).wait_send()
-        remote(
-            back_send.at[k], back_recv.at[k], back_ss.at[k], back_rs.at[k], at(me + devices - k)
-        ).wait_send()
+    stores.append(pltpu.make_async_copy(atm_surf, surf_to, out_sem.at[2]))
+    stores[2].start()
+    for copy in stores:
+        copy.wait()
+
+    settle(dst_send, dst_ss, 1, devices - 1)
+    settle(fwd_send, fwd_ss, 1, devices - 1)
+    settle(back_send, back_ss, 1, devices - 1)
+
+
+def hand_over(a, b, c, a_to, b_to, c_to, sem):
+    copies = [
+        pltpu.make_async_copy(src, dst, sem.at[n])
+        for n, (src, dst) in enumerate(((a, a_to), (b, b_to), (c, c_to)))
+    ]
+    for copy in copies:
+        copy.start()
+    for copy in copies:
+        copy.wait()
 
 
 def on_device(grps, tiles, *args):
@@ -395,18 +504,30 @@
     slots = 2 * devices
     vmem = pl.BlockSpec(memory_space=pltpu.VMEM)
     smem = pl.BlockSpec(memory_space=pltpu.SMEM)
+    far = pl.BlockSpec(memory_space=pl.ANY)
     chans, rows, cols = atmos.shape
     dma = pltpu.SemaphoreType.DMA
-    return pl.pallas_call(
+    shapes = (
+        jax.ShapeDtypeStruct(atmos.shape, F32),
+        jax.ShapeDtypeStruct(ocean.shape, F32),
+        jax.ShapeDtypeStruct((6, rows, cols), F32),
+    )
+    results = pl.pallas_call(
         functools.partial(kernel, grps, tiles),
-        out_shape=(
-            jax.ShapeDtypeStruct(atmos.shape, F32),
-            jax.ShapeDtypeStruct(ocean.shape, F32),
-            jax.ShapeDtypeStruct((6, rows, cols), F32),
-        ),
-        in_specs=[vmem, vmem, vmem, smem] + [vmem] * 9,
-        out_specs=(vmem, vmem, vmem),
+        out_shape=shapes,
+        in_specs=[far, far, far, smem, vmem, vmem, far, far, far, far, vmem, vmem, vmem],
+        out_specs=(far, far, far),
         scratch_shapes=[
+            pltpu.VMEM((chans, rows, cols), F32),
+            pltpu.VMEM((rows, cols), F32),
+            pltpu.VMEM((rows, cols), I32),
+            pltpu.VMEM(source_col.shape, I32),
+            pltpu.VMEM(source_col.shape, I32),
+            pltpu.VMEM(source_col.shape, F32),
+            pltpu.VMEM(ocean.shape, F32),
+            pltpu.VMEM((chans, rows, cols), F32),
+            pltpu.VMEM(ocean.shape, F32),
+            pltpu.VMEM((6, rows, cols), F32),
             pltpu.VMEM((chans, rows, cols), F32),
             pltpu.VMEM((2, 2, chans, cols), F32),
             pltpu.VMEM((2, 2, chans, cols), F32),
@@ -415,27 +536,33 @@
             pltpu.VMEM((slots, 128), F32),
             pltpu.VMEM((slots, 128), F32),
             pltpu.VMEM((slots, 128), F32),
-            pltpu.VMEM((slots, 128), F32),
+            pltpu.VMEM((devices, 2, 128), F32),
+            pltpu.VMEM((devices, 2, 128), F32),
+            pltpu.VMEM((devices, 2, 128), F32),
             pltpu.VMEM((slots, 128), F32),
             pltpu.VMEM((256, slots * 128), BF16),
             pltpu.VMEM((128, slots * 128), BF16),
             pltpu.VMEM((2, 192, 128), F32),
-            pltpu.VMEM((192, 512), BF16),
-            pltpu.VMEM((devices, 2, 16, 128), BF16),
-            pltpu.VMEM((devices, 2, 16, 128), BF16),
+            pltpu.VMEM((192, 256), BF16),
+            pltpu.VMEM((devices, 3, 8, 128), BF16),
+            pltpu.VMEM((devices, 3, 8, 128), BF16),
             pltpu.VMEM((128, G * 256), BF16),
             pltpu.VMEM((64, 128), F32),
-            pltpu.VMEM((devices, 16, 128), BF16),
-            pltpu.VMEM((devices, 16, 128), BF16),
+            pltpu.VMEM((devices, 3, 4, 128), BF16),
+            pltpu.VMEM((devices, 3, 4, 128), BF16),
             pltpu.VMEM((256, G * 256), BF16),
             pltpu.VMEM((128, 128), F32),
             pltpu.VMEM((256, 256), F32),
             dma((2, 4)),
             dma((2, 4)),
-            dma((devices,)),
-            dma((devices,)),
-            dma((devices,)),
-            dma((devices,)),
+            dma(()),
+            dma(()),
+            dma(()),
+            dma((devices // G,)),
+            dma(()),
+            dma((devices // G,)),
+            dma((11,)),
+            dma((3,)),
         ],
         compiler_params=pltpu.CompilerParams(
             collective_id=0, has_side_effects=True, vmem_limit_bytes=56 * 1024 * 1024
@@ -455,6 +582,13 @@
         couple,
         surface_weight,
     )
+    return pl.pallas_call(
+        hand_over,
+        out_shape=shapes,
+        in_specs=[far] * 3,
+        out_specs=(far, far, far),
+        scratch_shapes=[dma((3,))],
+    )(*results)
 
 
 def solution(mesh):

time: 69.7 us -> 67.1 us (0.963)
  local copies, waits for them, and re-layouts: 2.97 us -> 0 us
  Pallas kernels: 65.3 us -> 66.3 us
    unnamed x7 -> x0, local copies, waits for them, and re-layouts: 2.97 us -> none
    pallas_call x1 -> x2, Pallas kernels: 65.3 us -> 66.3 us  [the longest x1 53.3 us: on_device(): pl.pallas_call(functools.partial(kernel, grps, tiles), out_shape=shapes,...]
where the time goes in v2:
time: 67.1 us; the launch traced here: 67 us
  Pallas kernels  66.3 us (99%)
    pallas_call x1, Pallas kernels, on_device(): pl.pallas_call(functools.partial(kernel, grps, tiles), out_shape=shapes,...  53.3 us
    pallas_call x1, Pallas kernels, on_device(): pl.pallas_call(hand_over, out_shape=shapes, in_specs=[far] * 3, out_specs...  13 us

profile of v2, /device:TPU:1, one launch (start us, length us, event | category | flops | bytes accessed | tf_op | source)
XLA Modules:
  0.0 67.0 jit_solution(646223781147874383)
XLA Ops:
  0.6 53.3 %shard_map.148 = (f32[16,16,256]{2,1,0:T(8,128)}, f32[8,1024]{1,0:T(8,128)}, f32[6,16,256]{2,1,0:T(8,128)}) custom-call(f32[16,16,256]{2,1,0:T(8,128)} %atmos_in.1, f32[16,256]{1,0:T(8,128)} %kappa_in.1, s32[16,256]{1,0:T(8,128)} %sea_atm_in.1, f32[12,16]{1,0:T(8,128)} %flux_w.1, s32[1,128]{1,0:T(1,128)} %bitcast.4, s32[1,128]{1,0:T(1,128)} %bitcast.5, ...), custom_call_target="tpu_custom_call" | custom-call | tf_op jit(solution)/shard_map/pallas_call | solution.py:515
  53.9 13.0 %shard_map.149 = (f32[16,16,256]{2,1,0:T(8,128)}, f32[8,1024]{1,0:T(8,128)}, f32[6,16,256]{2,1,0:T(8,128)}) custom-call(f32[16,16,256]{2,1,0:T(8,128)} %get-tuple-element.6.a, f32[8,1024]{1,0:T(8,128)} %get-tuple-element.7.b, f32[6,16,256]{2,1,0:T(8,128)} %get-tuple-element.8.c), custom_call_target="tpu_custom_call" | custom-call | tf_op jit(solution)/shard_map/pallas_call | solution.py:585

commit v3 on v2

--- a/solution.py
+++ b/solution.py
@@ -125,39 +125,27 @@
         k = i * G + j
         return remote(back_send.at[k], back_recv.at[k], back_ss, back_rs.at[i], peer(i, j, True))
 
-    def others(i, act):
-        for j in range(G):
-            if j == 0:
-
-                @pl.when(i > 0)
-                def _():
-                    act(i, 0)
-            else:
-                act(i, j)
+    def each_group(act):
+        @pl.loop(1, groups)
+        def _(i):
+            act(i, 0)
+
+        act(0, 1)
 
     def settle(buffer, sem, start, size):
         part = buffer.at[pl.ds(start, size)]
         pltpu.make_async_copy(part, part, sem).wait()
 
-    def settle_group(buffer, sems, i):
-        @pl.when(i == 0)
-        def _():
-            settle(buffer, sems.at[0], 1, G - 1)
-
-        @pl.when(i > 0)
-        def _():
-            settle(buffer, sems.at[i], i * G, G)
+    def settle_group(buffer, sems, i, first):
+        settle(buffer, sems.at[i], i * G + first, G - first)
 
     barrier = pltpu.get_barrier_semaphore()
 
-    @pl.loop(0, groups)
-    def _(i):
-        others(
-            i,
-            lambda i, j: pl.semaphore_signal(
-                barrier, inc=1, device_id=peer(i, j), device_id_type=MESH
-            ),
-        )
+    def greet(i, first):
+        for j in range(first, G):
+            pl.semaphore_signal(barrier, inc=1, device_id=peer(i, j), device_id_type=MESH)
+
+    each_group(greet)
 
     loads = {}
     for n, (name, a, b) in enumerate(
@@ -174,64 +162,66 @@
         loads[name] = pltpu.make_async_copy(a, b, in_sem.at[n])
         loads[name].start()
 
-    blocks = owner.shape[1]
-    own_row = owner[...]
-    own_here = jnp.broadcast_to(own_row, (blocks, blocks)).astype(F32)
-    own_col = jnp.transpose(own_here)
-    cnt_col = jnp.transpose(jnp.broadcast_to(count[...], (blocks, blocks)).astype(F32))
-    before = iota((blocks, blocks), 0) < iota((blocks, blocks), 1)
-    same = jnp.where((own_here == own_col) & before, F32(1), F32(0))
-    rank = jnp.sum(same, axis=0, keepdims=True).astype(I32)
-    dx = ((own_row >> 5) - g) & 3
-    dz = (((own_row >> 3) & 3) - z - dx) & 3
-    dy = (((own_row >> 1) & 3) - y - dx) & 3
-    dc = ((own_row & 1) - core) & 1
-    slot = (((dz * 4 + dy) * 4 + dx) * 2 + dc) * 2 + rank
-    place = jnp.where(
-        iota((2 * devices, blocks), 0) == jnp.broadcast_to(slot, (2 * devices, blocks)), F32(1), F32(0)
-    ).astype(BF16)
-
-    def placed(values):
-        return jnp.dot(place, values.astype(BF16), preferred_element_type=F32)
-
-    for name in ("source", "dest", "margin"):
-        loads[name].wait()
-    src = source[...]
-    src_hi[...] = placed((src >> 8).astype(F32))
-    src_lo[...] = placed((src & 255).astype(F32))
-    dst = dest[...]
-    dst_all[...] = placed((dst >> 7).astype(F32)) * 128.0 + placed((dst & 127).astype(F32))
-
-    @pl.loop(0, devices // 4)
-    def _(i):
-        four = dst_all[pl.ds(pl.multiple_of(i * 8, 8), 8), :]
-        for j in range(4):
-            dst_send[i * 4 + j] = four[2 * j : 2 * j + 2]
-
-    dst_recv[0] = dst_send[0]
-    lanes = iota((blocks, 128), 1).astype(F32)
-    live = jnp.where(lanes < cnt_col[:, :1], margin[...], F32(0))
-    first = live.astype(BF16).astype(F32)
-    rest = live - first
-    second = rest.astype(BF16).astype(F32)
-    third = rest - second
-    weight[...] = placed(first) + placed(second) + placed(third)
+    for load in loads.values():
+        load.wait()
 
     ids16 = (iota((16, 16, 128), 0) * 16 + iota((16, 16, 128), 1)).astype(F32).astype(BF16)
     ids8 = (iota((8, 16, 128), 0) * 16 + iota((8, 16, 128), 1)).astype(F32).astype(BF16)
     one, zero = jnp.ones((16, 128), BF16), jnp.zeros((16, 128), BF16)
 
-    @pl.loop(0, devices // 4)
-    def _(i):
-        low = src_lo[pl.ds(pl.multiple_of(i * 8, 8), 8), :]
-        for j in range(8):
-            lo = rows_of(low[j : j + 1], 16).astype(BF16)
-            hot = jnp.where(ids16 == lo[None], one[None], zero[None])
-            hot_src[:, pl.ds(pl.multiple_of(i * 1024 + j * 128, 128), 128)] = hot.reshape(256, 128)
-
-    for name in ("atmos", "kappa", "sea", "ocean"):
-        loads[name].wait()
-    pl.semaphore_wait(barrier, devices - 1)
+    def place_blocks():
+        blocks = owner.shape[1]
+        own_row = owner[...]
+        own_here = jnp.broadcast_to(own_row, (blocks, blocks)).astype(F32)
+        own_col = jnp.transpose(own_here)
+        cnt_col = jnp.transpose(jnp.broadcast_to(count[...], (blocks, blocks)).astype(F32))
+        before = iota((blocks, blocks), 0) < iota((blocks, blocks), 1)
+        same = jnp.where((own_here == own_col) & before, F32(1), F32(0))
+        rank = jnp.sum(same, axis=0, keepdims=True).astype(I32)
+        dx = ((own_row >> 5) - g) & 3
+        dz = (((own_row >> 3) & 3) - z - dx) & 3
+        dy = (((own_row >> 1) & 3) - y - dx) & 3
+        dc = ((own_row & 1) - core) & 1
+        slot = (((dz * 4 + dy) * 4 + dx) * 2 + dc) * 2 + rank
+        place = jnp.where(
+            iota((2 * devices, blocks), 0) == jnp.broadcast_to(slot, (2 * devices, blocks)), F32(1), F32(0)
+        ).astype(BF16)
+
+        def placed(values):
+            return jnp.dot(place, values.astype(BF16), preferred_element_type=F32)
+
+        src = source[...]
+        src_hi[...] = placed((src >> 8).astype(F32))
+        src_lo[...] = placed((src & 255).astype(F32))
+        dst = dest[...]
+        dst_all[...] = placed((dst >> 7).astype(F32)) * 128.0 + placed((dst & 127).astype(F32))
+
+        @pl.loop(0, devices // 4)
+        def _(i):
+            four = dst_all[pl.ds(pl.multiple_of(i * 8, 8), 8), :]
+            for j in range(4):
+                dst_send[i * 4 + j] = four[2 * j : 2 * j + 2]
+
+        dst_recv[0] = dst_send[0]
+        lanes = iota((blocks, 128), 1).astype(F32)
+        live = jnp.where(lanes < cnt_col[:, :1], margin[...], F32(0))
+        first = live.astype(BF16).astype(F32)
+        rest = live - first
+        second = rest.astype(BF16).astype(F32)
+        third = rest - second
+        weight[...] = placed(first) + placed(second) + placed(third)
+
+    def hot_source(i, first):
+        here = pl.ds(pl.multiple_of(i * 2 * G, 2 * G), 2 * G)
+        low = src_lo[here, :]
+        for j in range(G):
+            for part in range(2):
+                lo = rows_of(low[2 * j + part : 2 * j + part + 1], 16).astype(BF16)
+                hot = jnp.where(ids16 == lo[None], one[None], zero[None])
+                at = pl.multiple_of(i * width + j * 256 + part * 128, 128)
+                hot_src[:, pl.ds(at, 128)] = hot.reshape(256, 128)
+            if j >= first:
+                dest_copy(i, j).start()
 
     rows, cols = atmos.shape[1], atmos.shape[2]
     chans = atmos.shape[0]
@@ -269,13 +259,23 @@
                     beside[side],
                 )
             )
+        if step == 0:
+            pl.semaphore_wait(barrier, devices - 1)
         for copy in copies:
             copy.start()
         if step == 0:
-
-            @pl.loop(0, groups)
+            place_blocks()
+
+            @pl.loop(1, groups // 2)
             def _(i):
-                others(i, lambda i, j: dest_copy(i, j).start())
+                hot_source(i, 0)
+
+            hot_source(0, 1)
+        else:
+
+            @pl.loop(groups // 2, groups)
+            def _(i):
+                hot_source(i, 0)
 
         for copy in copies:
             copy.wait()
@@ -317,8 +317,7 @@
     sub = iota((8, 128), 0)
     odd = jnp.where(sub >= 4, F32(1), F32(0))
 
-    @pl.loop(0, groups)
-    def _(i):
+    def give(i, first):
         here = pl.ds(pl.multiple_of(i * 2 * G, 2 * G), 2 * G)
         hi, w = src_hi[here, :], weight[here, :]
         for j in range(G):
@@ -339,7 +338,10 @@
                 fwd_send[i * G + j, part] = (wide * scale).astype(BF16)
                 ends.append((thin + pltpu.roll(thin, 4, 0)) * scale)
             fwd_send[i * G + j, 2] = jnp.where(sub < 4, ends[0], ends[1]).astype(BF16)
-        others(i, lambda i, j: fwd_copy(i, j).start())
+            if j >= first:
+                fwd_copy(i, j).start()
+
+    each_group(give)
 
     fwd_recv[0] = fwd_send[0]
 
@@ -361,9 +363,8 @@
 
     total[...] = jnp.zeros_like(total)
 
-    @pl.loop(0, groups)
-    def _(i):
-        settle_group(fwd_recv, fwd_rs, i)
+    def collect(i, first):
+        settle_group(fwd_recv, fwd_rs, i, first)
         for j in range(G):
             high = dst_hi[i * G + j]
             ends = fwd_recv[i * G + j, 2].astype(F32)
@@ -383,6 +384,8 @@
             preferred_element_type=F32,
         )
 
+    each_group(collect)
+
     surf32[...] = jnp.zeros_like(surf32)
     for h in range(8):
         here = slice(h * 128, h * 128 + 128)
@@ -400,8 +403,7 @@
     stores.append(pltpu.make_async_copy(ocean_out, ocean_to, out_sem.at[1]))
     stores[1].start()
 
-    @pl.loop(0, groups)
-    def _(i):
+    def answer(i, first):
         for j in range(G):
             k = i * G + j
             found = jnp.dot(
@@ -421,15 +423,17 @@
                 both.append(got)
             ends = jnp.where(sub < 2, pltpu.roll(both[0], 4, 0), pltpu.roll(both[1], 6, 0))
             back_send[k, 2] = ends[0:4].astype(BF16)
-        others(i, lambda i, j: back_copy(i, j).start())
+            if j >= first:
+                back_copy(i, j).start()
+
+    each_group(answer)
 
     back_recv[0] = back_send[0]
 
     summed[...] = jnp.zeros_like(summed)
 
-    @pl.loop(0, groups)
-    def _(i):
-        settle_group(back_recv, back_rs, i)
+    def gather_up(i, first):
+        settle_group(back_recv, back_rs, i, first)
         here = pl.ds(pl.multiple_of(i * 2 * G, 2 * G), 2 * G)
         hi, w = src_hi[here, :], weight[here, :]
         for j in range(G):
@@ -439,28 +443,28 @@
                 last = [ends[2:4], ends[0:2]] if part else [ends]
                 value = jnp.concatenate([most] + last, axis=0)
                 value = value * rows_of(w[2 * j + part : 2 * j + part + 1], 8)
-                top = value.astype(BF16).astype(F32)
-                pair = jnp.concatenate([top, value - top], axis=0).astype(BF16)
-                h = rows_of(hi[2 * j + part : 2 * j + part + 1], 16).astype(BF16)
+                pair = jnp.concatenate([value, value], axis=0).astype(BF16)
+                h = (rows_of(hi[2 * j + part : 2 * j + part + 1], 16) - upper).astype(BF16)
                 at = slice(j * 256 + part * 128, j * 256 + part * 128 + 128)
-                for v in range(16):
-                    spread2[v * 16 : v * 16 + 16, at] = jnp.where(h == v, pair, zero)
-        summed[...] += lax.dot_general(
+                for v in range(8):
+                    spread2[v * 16 : v * 16 + 16, at] = jnp.where(h == 2 * v, pair, zero)
+        added = lax.dot_general(
             spread2[...],
             hot_src[:, pl.ds(pl.multiple_of(i * width, width), width)],
             NT,
             preferred_element_type=F32,
         )
+        summed[0] += added[:, 0:128]
+        summed[1] += added[:, 128:256]
+
+    upper = jnp.where(iota((16, 128), 0) >= 8, F32(1), F32(0))
+    each_group(gather_up)
 
     for half in range(2):
         here = slice(half * 128, half * 128 + 128)
-        for h in range(16):
-            table32[half, h * 8 : h * 8 + 8, :] = (
-                summed[h * 16 : h * 16 + 8, here] + summed[h * 16 + 8 : h * 16 + 16, here]
-            )
         for s in range(6):
             atm_surf[s, :, here] = jnp.where(
-                sea[:, here], table32[half, pl.ds(s, 16, stride=8), :], F32(0)
+                sea[:, here], summed[half, pl.ds(s, 16, stride=8), :], F32(0)
             )
 
     stores.append(pltpu.make_async_copy(atm_surf, surf_to, out_sem.at[2]))
@@ -473,14 +477,18 @@
     settle(back_send, back_ss, 1, devices - 1)
 
 
-def hand_over(a, b, c, a_to, b_to, c_to, sem):
-    copies = [
-        pltpu.make_async_copy(src, dst, sem.at[n])
-        for n, (src, dst) in enumerate(((a, a_to), (b, b_to), (c, c_to)))
-    ]
-    for copy in copies:
+def hand_over(a, b, c, a_to, b_to, c_to, a_here, b_here, c_here, sem):
+    here = (a_here.at[pl.ds(0, 8)], a_here.at[pl.ds(8, 8)], b_here, c_here)
+    into = (a.at[pl.ds(0, 8)], a.at[pl.ds(8, 8)], b, c)
+    out = (a_to.at[pl.ds(0, 8)], a_to.at[pl.ds(8, 8)], b_to, c_to)
+    loads = [pltpu.make_async_copy(into[n], here[n], sem.at[n]) for n in range(4)]
+    stores = [pltpu.make_async_copy(here[n], out[n], sem.at[4 + n]) for n in range(4)]
+    for copy in loads:
         copy.start()
-    for copy in copies:
+    for n in range(4):
+        loads[n].wait()
+        stores[n].start()
+    for copy in stores:
         copy.wait()
 
 
@@ -550,9 +558,9 @@
             pltpu.VMEM((64, 128), F32),
             pltpu.VMEM((devices, 3, 4, 128), BF16),
             pltpu.VMEM((devices, 3, 4, 128), BF16),
-            pltpu.VMEM((256, G * 256), BF16),
+            pltpu.VMEM((128, G * 256), BF16),
             pltpu.VMEM((128, 128), F32),
-            pltpu.VMEM((256, 256), F32),
+            pltpu.VMEM((2, 128, 128), F32),
             dma((2, 4)),
             dma((2, 4)),
             dma(()),
@@ -587,7 +595,7 @@
         out_shape=shapes,
         in_specs=[far] * 3,
         out_specs=(far, far, far),
-        scratch_shapes=[dma((3,))],
+        scratch_shapes=[pltpu.VMEM(x.shape, F32) for x in shapes] + [dma((8,))],
     )(*results)
 
 

time: 67.1 us -> 85.6 us (1.28); the launches traced: 67 us -> 83.9 us
  Pallas kernels: 66.3 us -> 83.3 us
    pallas_call x1, Pallas kernels: 53.3 us -> 81.5 us  [on_device(): pl.pallas_call(functools.partial(kernel, grps, tiles), out_shape=shapes,...]
    pallas_call x1, Pallas kernels: 13 us -> 1.75 us  [on_device(): pl.pallas_call(hand_over, out_shape=shapes, in_specs=[far] * 3, out_specs...]
where the time goes in v3:
time: 85.6 us; the launch traced here: 83.9 us
  Pallas kernels  83.3 us (97%)
    pallas_call x1, Pallas kernels, on_device(): pl.pallas_call(functools.partial(kernel, grps, tiles), out_shape=shapes,...  81.5 us
    pallas_call x1, Pallas kernels, on_device(): pl.pallas_call(hand_over, out_shape=shapes, in_specs=[far] * 3, out_specs...  1.75 us

profile of v3, /device:TPU:1, one launch (start us, length us, event | category | flops | bytes accessed | tf_op | source)
XLA Modules:
  0.0 83.9 jit_solution(13579236463090631495)
XLA Ops:
  0.6 81.5 %shard_map.148 = (f32[16,16,256]{2,1,0:T(8,128)}, f32[8,1024]{1,0:T(8,128)}, f32[6,16,256]{2,1,0:T(8,128)}) custom-call(f32[16,16,256]{2,1,0:T(8,128)} %atmos_in.1, f32[16,256]{1,0:T(8,128)} %kappa_in.1, s32[16,256]{1,0:T(8,128)} %sea_atm_in.1, f32[12,16]{1,0:T(8,128)} %flux_w.1, s32[1,128]{1,0:T(1,128)} %bitcast.4, s32[1,128]{1,0:T(1,128)} %bitcast.5, ...), custom_call_target="tpu_custom_call" | custom-call | tf_op jit(solution)/shard_map/pallas_call | solution.py:523
  82.2 1.7 %shard_map.149 = (f32[16,16,256]{2,1,0:T(8,128)}, f32[8,1024]{1,0:T(8,128)}, f32[6,16,256]{2,1,0:T(8,128)}) custom-call(f32[16,16,256]{2,1,0:T(8,128)} %get-tuple-element.6.a, f32[8,1024]{1,0:T(8,128)} %get-tuple-element.7.b, f32[6,16,256]{2,1,0:T(8,128)} %get-tuple-element.8.c), custom_call_target="tpu_custom_call" | custom-call | tf_op jit(solution)/shard_map/pallas_call | solution.py:593

commit v4 on v3

--- a/solution.py
+++ b/solution.py
@@ -132,6 +132,13 @@
 
         act(0, 1)
 
+    def start_all(make):
+        def act(i, first):
+            for j in range(first, G):
+                make(i, j).start()
+
+        return act
+
     def settle(buffer, sem, start, size):
         part = buffer.at[pl.ds(start, size)]
         pltpu.make_async_copy(part, part, sem).wait()
@@ -211,7 +218,7 @@
         third = rest - second
         weight[...] = placed(first) + placed(second) + placed(third)
 
-    def hot_source(i, first):
+    def hot_source(i):
         here = pl.ds(pl.multiple_of(i * 2 * G, 2 * G), 2 * G)
         low = src_lo[here, :]
         for j in range(G):
@@ -220,8 +227,6 @@
                 hot = jnp.where(ids16 == lo[None], one[None], zero[None])
                 at = pl.multiple_of(i * width + j * 256 + part * 128, 128)
                 hot_src[:, pl.ds(at, 128)] = hot.reshape(256, 128)
-            if j >= first:
-                dest_copy(i, j).start()
 
     rows, cols = atmos.shape[1], atmos.shape[2]
     chans = atmos.shape[0]
@@ -265,17 +270,12 @@
             copy.start()
         if step == 0:
             place_blocks()
-
-            @pl.loop(1, groups // 2)
+            each_group(start_all(dest_copy))
+        else:
+
+            @pl.loop(0, groups)
             def _(i):
-                hot_source(i, 0)
-
-            hot_source(0, 1)
-        else:
-
-            @pl.loop(groups // 2, groups)
-            def _(i):
-                hot_source(i, 0)
+                hot_source(i)
 
         for copy in copies:
             copy.wait()
@@ -338,8 +338,7 @@
                 fwd_send[i * G + j, part] = (wide * scale).astype(BF16)
                 ends.append((thin + pltpu.roll(thin, 4, 0)) * scale)
             fwd_send[i * G + j, 2] = jnp.where(sub < 4, ends[0], ends[1]).astype(BF16)
-            if j >= first:
-                fwd_copy(i, j).start()
+        start_all(fwd_copy)(i, first)
 
     each_group(give)
 
@@ -423,8 +422,7 @@
                 both.append(got)
             ends = jnp.where(sub < 2, pltpu.roll(both[0], 4, 0), pltpu.roll(both[1], 6, 0))
             back_send[k, 2] = ends[0:4].astype(BF16)
-            if j >= first:
-                back_copy(i, j).start()
+        start_all(back_copy)(i, first)
 
     each_group(answer)
 
@@ -443,28 +441,31 @@
                 last = [ends[2:4], ends[0:2]] if part else [ends]
                 value = jnp.concatenate([most] + last, axis=0)
                 value = value * rows_of(w[2 * j + part : 2 * j + part + 1], 8)
-                pair = jnp.concatenate([value, value], axis=0).astype(BF16)
-                h = (rows_of(hi[2 * j + part : 2 * j + part + 1], 16) - upper).astype(BF16)
+                top = value.astype(BF16).astype(F32)
+                pair = jnp.concatenate([top, value - top], axis=0).astype(BF16)
+                h = rows_of(hi[2 * j + part : 2 * j + part + 1], 16).astype(BF16)
                 at = slice(j * 256 + part * 128, j * 256 + part * 128 + 128)
-                for v in range(8):
-                    spread2[v * 16 : v * 16 + 16, at] = jnp.where(h == 2 * v, pair, zero)
+                for v in range(16):
+                    spread2[v * 16 : v * 16 + 16, at] = jnp.where(h == v, pair, zero)
         added = lax.dot_general(
             spread2[...],
             hot_src[:, pl.ds(pl.multiple_of(i * width, width), width)],
             NT,
             preferred_element_type=F32,
         )
-        summed[0] += added[:, 0:128]
-        summed[1] += added[:, 128:256]
-
-    upper = jnp.where(iota((16, 128), 0) >= 8, F32(1), F32(0))
+        summed[...] += added
+
     each_group(gather_up)
 
     for half in range(2):
         here = slice(half * 128, half * 128 + 128)
+        for h in range(16):
+            table32[half, h * 8 : h * 8 + 8, :] = (
+                summed[h * 16 : h * 16 + 8, here] + summed[h * 16 + 8 : h * 16 + 16, here]
+            )
         for s in range(6):
             atm_surf[s, :, here] = jnp.where(
-                sea[:, here], summed[half, pl.ds(s, 16, stride=8), :], F32(0)
+                sea[:, here], table32[half, pl.ds(s, 16, stride=8), :], F32(0)
             )
 
     stores.append(pltpu.make_async_copy(atm_surf, surf_to, out_sem.at[2]))
@@ -558,9 +559,9 @@
             pltpu.VMEM((64, 128), F32),
             pltpu.VMEM((devices, 3, 4, 128), BF16),
             pltpu.VMEM((devices, 3, 4, 128), BF16),
-            pltpu.VMEM((128, G * 256), BF16),
+            pltpu.VMEM((256, G * 256), BF16),
             pltpu.VMEM((128, 128), F32),
-            pltpu.VMEM((2, 128, 128), F32),
+            pltpu.VMEM((256, 256), F32),
             dma((2, 4)),
             dma((2, 4)),
             dma(()),

time: 85.6 us -> 53.2 us (0.62); the launches traced: 83.9 us -> 53 us
  Pallas kernels: 83.3 us -> 52.3 us
    pallas_call x1, Pallas kernels: 81.5 us -> 50.6 us  [on_device(): pl.pallas_call(functools.partial(kernel, grps, tiles), out_shape=shapes,...]
where the time goes in v4:
time: 53.2 us; the launch traced here: 53 us
  Pallas kernels  52.3 us (98%)
  between operations  0.64 us (1%)
    pallas_call x1, Pallas kernels, on_device(): pl.pallas_call(functools.partial(kernel, grps, tiles), out_shape=shapes,...  50.6 us
    pallas_call x1, Pallas kernels, on_device(): pl.pallas_call(hand_over, out_shape=shapes, in_specs=[far] * 3, out_specs...  1.75 us

profile of v4, /device:TPU:1, one launch (start us, length us, event | category | flops | bytes accessed | tf_op | source)
XLA Modules:
  0.0 53.0 jit_solution(6507670637674081310)
XLA Ops:
  0.6 50.6 %shard_map.148 = (f32[16,16,256]{2,1,0:T(8,128)}, f32[8,1024]{1,0:T(8,128)}, f32[6,16,256]{2,1,0:T(8,128)}) custom-call(f32[16,16,256]{2,1,0:T(8,128)} %atmos_in.1, f32[16,256]{1,0:T(8,128)} %kappa_in.1, s32[16,256]{1,0:T(8,128)} %sea_atm_in.1, f32[12,16]{1,0:T(8,128)} %flux_w.1, s32[1,128]{1,0:T(1,128)} %bitcast.4, s32[1,128]{1,0:T(1,128)} %bitcast.5, ...), custom_call_target="tpu_custom_call" | custom-call | tf_op jit(solution)/shard_map/pallas_call | solution.py:524
  51.2 1.7 %shard_map.149 = (f32[16,16,256]{2,1,0:T(8,128)}, f32[8,1024]{1,0:T(8,128)}, f32[6,16,256]{2,1,0:T(8,128)}) custom-call(f32[16,16,256]{2,1,0:T(8,128)} %get-tuple-element.6.a, f32[8,1024]{1,0:T(8,128)} %get-tuple-element.7.b, f32[6,16,256]{2,1,0:T(8,128)} %get-tuple-element.8.c), custom_call_target="tpu_custom_call" | custom-call | tf_op jit(solution)/shard_map/pallas_call | solution.py:594

commit v5 on v4

--- a/solution.py
+++ b/solution.py
@@ -66,6 +66,7 @@
     row_recv,
     col_send,
     col_recv,
+    corner_recv,
     src_hi,
     src_lo,
     dst_all,
@@ -146,22 +147,14 @@
     def settle_group(buffer, sems, i, first):
         settle(buffer, sems.at[i], i * G + first, G - first)
 
-    barrier = pltpu.get_barrier_semaphore()
-
-    def greet(i, first):
-        for j in range(first, G):
-            pl.semaphore_signal(barrier, inc=1, device_id=peer(i, j), device_id_type=MESH)
-
-    each_group(greet)
-
     loads = {}
     for n, (name, a, b) in enumerate(
         (
+            ("atmos", atmos_in, atmos),
+            ("kappa", kappa_in, kappa),
             ("source", source_in, source),
             ("dest", dest_in, dest),
             ("margin", margin_in, margin),
-            ("atmos", atmos_in, atmos),
-            ("kappa", kappa_in, kappa),
             ("sea", sea_atm_in, sea_atm),
             ("ocean", ocean_in, ocean),
         )
@@ -169,8 +162,13 @@
         loads[name] = pltpu.make_async_copy(a, b, in_sem.at[n])
         loads[name].start()
 
-    for load in loads.values():
-        load.wait()
+    barrier = pltpu.get_barrier_semaphore()
+
+    def greet(i, first):
+        for j in range(first, G):
+            pl.semaphore_signal(barrier, inc=1, device_id=peer(i, j), device_id_type=MESH)
+
+    each_group(greet)
 
     ids16 = (iota((16, 16, 128), 0) * 16 + iota((16, 16, 128), 1)).astype(F32).astype(BF16)
     ids8 = (iota((8, 16, 128), 0) * 16 + iota((8, 16, 128), 1)).astype(F32).astype(BF16)
@@ -218,82 +216,148 @@
         third = rest - second
         weight[...] = placed(first) + placed(second) + placed(third)
 
-    def hot_source(i):
-        here = pl.ds(pl.multiple_of(i * 2 * G, 2 * G), 2 * G)
-        low = src_lo[here, :]
-        for j in range(G):
-            for part in range(2):
-                lo = rows_of(low[2 * j + part : 2 * j + part + 1], 16).astype(BF16)
-                hot = jnp.where(ids16 == lo[None], one[None], zero[None])
-                at = pl.multiple_of(i * width + j * 256 + part * 128, 128)
-                hot_src[:, pl.ds(at, 128)] = hot.reshape(256, 128)
-
     rows, cols = atmos.shape[1], atmos.shape[2]
     chans = atmos.shape[0]
     row_id, col_id = iota((rows, cols), 0), iota((rows, cols), 1)
     lane = iota((rows, 128), 1)
-    beside = (
-        (lax.rem(g + grps - 1, grps), t),
-        (lax.rem(g + 1, grps), t),
-        (g, lax.rem(t + tiles - 1, tiles)),
-        (g, lax.rem(t + 1, tiles)),
+    up_g, down_g = lax.rem(g + grps - 1, grps), lax.rem(g + 1, grps)
+    left_t, right_t = lax.rem(t + tiles - 1, tiles), lax.rem(t + 1, tiles)
+    edge_n, edge_s, edge_w, edge_e = g == 0, g == grps - 1, t == 0, t == tiles - 1
+    loads["atmos"].wait()
+    loads["kappa"].wait()
+    diffusion = kappa[...]
+    west = jnp.where(lane == 2 * chans, diffusion[:, 0:1], F32(0))
+    east = jnp.where(lane == 2 * chans, diffusion[:, cols - 1 : cols], F32(0))
+    for ch in range(chans):
+        x = atmos[ch]
+        far_ch = chans + ch
+        row_send[0, ch : ch + 1, :] = x[0:1]
+        row_send[0, far_ch : far_ch + 1, :] = x[1:2]
+        row_send[1, ch : ch + 1, :] = x[rows - 1 : rows]
+        row_send[1, far_ch : far_ch + 1, :] = x[rows - 2 : rows - 1]
+        west = jnp.where(lane == ch, x[:, 0:1], west)
+        west = jnp.where(lane == far_ch, x[:, 1:2], west)
+        east = jnp.where(lane == ch, x[:, cols - 1 : cols], east)
+        east = jnp.where(lane == far_ch, x[:, cols - 2 : cols - 1], east)
+    row_send[0, 2 * chans : 2 * chans + 1, :] = diffusion[0:1]
+    row_send[1, 2 * chans : 2 * chans + 1, :] = diffusion[rows - 1 : rows]
+    col_send[0] = west
+    col_send[1] = east
+    top, bottom = pl.ds(0, 8), pl.ds(rows - 8, 8)
+    plan = (
+        (row_send.at[0], row_recv.at[1], (up_g, t)),
+        (row_send.at[1], row_recv.at[0], (down_g, t)),
+        (col_send.at[0], col_recv.at[1], (g, left_t)),
+        (col_send.at[1], col_recv.at[0], (g, right_t)),
+        (col_send.at[0, top], corner_recv.at[3], (up_g, left_t)),
+        (col_send.at[1, top], corner_recv.at[2], (up_g, right_t)),
+        (col_send.at[0, bottom], corner_recv.at[1], (down_g, left_t)),
+        (col_send.at[1, bottom], corner_recv.at[0], (down_g, right_t)),
     )
-    edge = (g == 0, g == grps - 1, t == 0, t == tiles - 1)
-    diffusion = kappa[...]
+    copies = [
+        remote(src, dst, halo_ss.at[n], halo_rs.at[n], device)
+        for n, (src, dst, device) in enumerate(plan)
+    ]
+    pl.semaphore_wait(barrier, devices - 1)
+    for copy in copies:
+        copy.start()
+    for name in ("source", "dest", "margin", "sea", "ocean"):
+        loads[name].wait()
+    place_blocks()
+    each_group(start_all(dest_copy))
+    for copy in copies:
+        copy.wait()
+
+    nw = jnp.where(edge_n | edge_w, F32(0), corner_recv[0, 7:8, :])
+    ne = jnp.where(edge_n | edge_e, F32(0), corner_recv[1, 7:8, :])
+    sw = jnp.where(edge_s | edge_w, F32(0), corner_recv[2, 0:1, :])
+    se = jnp.where(edge_s | edge_e, F32(0), corner_recv[3, 0:1, :])
+
+    def upright(row):
+        spot = jnp.where(lane == iota((rows, 128), 0), jnp.broadcast_to(row, (rows, 128)), F32(0))
+        return jnp.sum(spot, axis=1, keepdims=True)
+
+    def line(here, below, above, at_left, at_right, rate):
+        left = jnp.where(col_id == 0, upright(at_left), pltpu.roll(here, 1, 1))
+        right = jnp.where(col_id == cols - 1, upright(at_right), pltpu.roll(here, cols - 1, 1))
+        return here + rate * (below + above + right + left - 4.0 * here)
+
+    row_lane = iota((rows, 128), 0)
+
+    def column(here, right, left, at_top, at_bottom, rate):
+        above = jnp.where(row_lane == 0, at_top, pltpu.roll(here, 1, 0))
+        below = jnp.where(row_lane == rows - 1, at_bottom, pltpu.roll(here, rows - 1, 0))
+        return here + rate * (below + above + right + left - 4.0 * here)
+
+    north = jnp.where(edge_n, F32(0), row_recv[0, 0:chans, :])
+    north2 = jnp.where(edge_n, F32(0), row_recv[0, chans : 2 * chans, :])
+    south = jnp.where(edge_s, F32(0), row_recv[1, 0:chans, :])
+    south2 = jnp.where(edge_s, F32(0), row_recv[1, chans : 2 * chans, :])
+    west = jnp.where(edge_w, F32(0), col_recv[0])
+    east = jnp.where(edge_e, F32(0), col_recv[1])
+    rim = [
+        (north, south, west, east),
+        (
+            jnp.where(
+                edge_n,
+                F32(0),
+                line(
+                    north,
+                    row_send[0, 0:chans, :],
+                    north2,
+                    nw,
+                    ne,
+                    row_recv[0, 2 * chans : 2 * chans + 1, :],
+                ),
+            ),
+            jnp.where(
+                edge_s,
+                F32(0),
+                line(
+                    south,
+                    south2,
+                    row_send[1, 0:chans, :],
+                    sw,
+                    se,
+                    row_recv[1, 2 * chans : 2 * chans + 1, :],
+                ),
+            ),
+            jnp.where(
+                edge_w,
+                F32(0),
+                column(
+                    west,
+                    col_send[0],
+                    pltpu.roll(west, 128 - chans, 1),
+                    nw,
+                    sw,
+                    col_recv[0, :, 2 * chans : 2 * chans + 1],
+                ),
+            ),
+            jnp.where(
+                edge_e,
+                F32(0),
+                column(
+                    east,
+                    pltpu.roll(east, 128 - chans, 1),
+                    col_send[1],
+                    ne,
+                    se,
+                    col_recv[1, :, 2 * chans : 2 * chans + 1],
+                ),
+            ),
+        ),
+    ]
     for step in range(2):
-        state = atmos if step == 0 else mid
-        west = jnp.zeros((rows, 128), F32)
-        east = jnp.zeros((rows, 128), F32)
-        for ch in range(chans):
-            x = state[ch]
-            row_send[step, 0, ch : ch + 1, :] = x[0:1]
-            row_send[step, 1, ch : ch + 1, :] = x[rows - 1 : rows]
-            west = jnp.where(lane == ch, x[:, 0:1], west)
-            east = jnp.where(lane == ch, x[:, cols - 1 : cols], east)
-        col_send[step, 0] = west
-        col_send[step, 1] = east
-        copies = []
-        for side in range(4):
-            sent, got = (row_send, row_recv) if side < 2 else (col_send, col_recv)
-            copies.append(
-                remote(
-                    sent.at[step, side % 2],
-                    got.at[step, 1 - side % 2],
-                    halo_ss.at[step, side],
-                    halo_rs.at[step, side],
-                    beside[side],
-                )
-            )
-        if step == 0:
-            pl.semaphore_wait(barrier, devices - 1)
-        for copy in copies:
-            copy.start()
-        if step == 0:
-            place_blocks()
-            each_group(start_all(dest_copy))
-        else:
-
-            @pl.loop(0, groups)
-            def _(i):
-                hot_source(i)
-
-        for copy in copies:
-            copy.wait()
-        north = jnp.where(edge[0], F32(0), row_recv[step, 0])
-        south = jnp.where(edge[1], F32(0), row_recv[step, 1])
-        west = jnp.where(edge[2], F32(0), col_recv[step, 0])
-        east = jnp.where(edge[3], F32(0), col_recv[step, 1])
+        state, after = (atmos, mid) if step == 0 else (mid, atmos_out)
+        north, south, west, east = rim[step]
         for ch in range(chans):
             x = state[ch]
             up = jnp.where(row_id == 0, north[ch : ch + 1], pltpu.roll(x, 1, 0))
             down = jnp.where(row_id == rows - 1, south[ch : ch + 1], pltpu.roll(x, rows - 1, 0))
             left = jnp.where(col_id == 0, west[:, ch : ch + 1], pltpu.roll(x, 1, 1))
             right = jnp.where(col_id == cols - 1, east[:, ch : ch + 1], pltpu.roll(x, cols - 1, 1))
-            new = x + diffusion * (down + up + right + left - 4.0 * x)
-            if step == 0:
-                mid[ch] = new
-            else:
-                atmos_out[ch] = new
+            after[ch] = x + diffusion * (down + up + right + left - 4.0 * x)
 
     stores = [pltpu.make_async_copy(atmos_out, atmos_to, out_sem.at[0])]
     stores[0].start()
@@ -319,9 +383,15 @@
 
     def give(i, first):
         here = pl.ds(pl.multiple_of(i * 2 * G, 2 * G), 2 * G)
+        low = src_lo[here, :]
         hi, w = src_hi[here, :], weight[here, :]
         for j in range(G):
-            hot = hot_src[:, pl.ds(pl.multiple_of(i * width + j * 256, 256), 256)]
+            hots = []
+            for part in range(2):
+                lo = rows_of(low[2 * j + part : 2 * j + part + 1], 16).astype(BF16)
+                hots.append(jnp.where(ids16 == lo[None], one[None], zero[None]).reshape(256, 128))
+            hot = jnp.concatenate(hots, axis=1)
+            hot_src[:, pl.ds(pl.multiple_of(i * width + j * 256, 256), 256)] = hot
             found = jnp.dot(table[...], hot, preferred_element_type=F32)
             ends = []
             for part in range(2):
@@ -538,10 +608,11 @@
             pltpu.VMEM(ocean.shape, F32),
             pltpu.VMEM((6, rows, cols), F32),
             pltpu.VMEM((chans, rows, cols), F32),
-            pltpu.VMEM((2, 2, chans, cols), F32),
-            pltpu.VMEM((2, 2, chans, cols), F32),
-            pltpu.VMEM((2, 2, rows, 128), F32),
-            pltpu.VMEM((2, 2, rows, 128), F32),
+            pltpu.VMEM((2, 2 * chans + 1, cols), F32),
+            pltpu.VMEM((2, 2 * chans + 1, cols), F32),
+            pltpu.VMEM((2, rows, 128), F32),
+            pltpu.VMEM((2, rows, 128), F32),
+            pltpu.VMEM((4, 8, 128), F32),
             pltpu.VMEM((slots, 128), F32),
             pltpu.VMEM((slots, 128), F32),
             pltpu.VMEM((slots, 128), F32),
@@ -562,8 +633,8 @@
             pltpu.VMEM((256, G * 256), BF16),
             pltpu.VMEM((128, 128), F32),
             pltpu.VMEM((256, 256), F32),
-            dma((2, 4)),
-            dma((2, 4)),
+            dma((8,)),
+            dma((8,)),
             dma(()),
             dma(()),
             dma(()),

time: 53.2 us -> 50.5 us (0.949)
  Pallas kernels: 52.3 us -> 49.7 us
    pallas_call x1, Pallas kernels: 50.6 us -> 47.9 us  [on_device(): pl.pallas_call(functools.partial(kernel, grps, tiles), out_shape=shapes,...]
where the time goes in v5:
time: 50.5 us; the launch traced here: 50.3 us
  Pallas kernels  49.7 us (98%)
  between operations  0.64 us (1%)
    pallas_call x1, Pallas kernels, on_device(): pl.pallas_call(functools.partial(kernel, grps, tiles), out_shape=shapes,...  47.9 us
    pallas_call x1, Pallas kernels, on_device(): pl.pallas_call(hand_over, out_shape=shapes, in_specs=[far] * 3, out_specs...  1.75 us

profile of v5, /device:TPU:1, one launch (start us, length us, event | category | flops | bytes accessed | tf_op | source)
XLA Modules:
  0.0 50.3 jit_solution(10875580463528560325)
XLA Ops:
  0.6 47.9 %shard_map.148 = (f32[16,16,256]{2,1,0:T(8,128)}, f32[8,1024]{1,0:T(8,128)}, f32[6,16,256]{2,1,0:T(8,128)}) custom-call(f32[16,16,256]{2,1,0:T(8,128)} %atmos_in.1, f32[16,256]{1,0:T(8,128)} %kappa_in.1, s32[16,256]{1,0:T(8,128)} %sea_atm_in.1, f32[12,16]{1,0:T(8,128)} %flux_w.1, s32[1,128]{1,0:T(1,128)} %bitcast.4, s32[1,128]{1,0:T(1,128)} %bitcast.5, ...), custom_call_target="tpu_custom_call" | custom-call | tf_op jit(solution)/shard_map/pallas_call | solution.py:594
  48.6 1.7 %shard_map.149 = (f32[16,16,256]{2,1,0:T(8,128)}, f32[8,1024]{1,0:T(8,128)}, f32[6,16,256]{2,1,0:T(8,128)}) custom-call(f32[16,16,256]{2,1,0:T(8,128)} %get-tuple-element.6.a, f32[8,1024]{1,0:T(8,128)} %get-tuple-element.7.b, f32[6,16,256]{2,1,0:T(8,128)} %get-tuple-element.8.c), custom_call_target="tpu_custom_call" | custom-call | tf_op jit(solution)/shard_map/pallas_call | solution.py:665

commit v6 on v5

--- a/solution.py
+++ b/solution.py
@@ -85,6 +85,7 @@
     back_send,
     back_recv,
     spread2,
+    spread3,
     total,
     summed,
     halo_ss,
@@ -500,8 +501,7 @@
 
     summed[...] = jnp.zeros_like(summed)
 
-    def gather_up(i, first):
-        settle_group(back_recv, back_rs, i, first)
+    def gather_up(i, spread2):
         here = pl.ds(pl.multiple_of(i * 2 * G, 2 * G), 2 * G)
         hi, w = src_hi[here, :], weight[here, :]
         for j in range(G):
@@ -525,7 +525,17 @@
         )
         summed[...] += added
 
-    each_group(gather_up)
+    @pl.loop(0, groups // 2 - 1)
+    def _(n):
+        settle_group(back_recv, back_rs, 2 * n + 1, 0)
+        settle_group(back_recv, back_rs, 2 * n + 2, 0)
+        gather_up(2 * n + 1, spread2)
+        gather_up(2 * n + 2, spread3)
+
+    settle_group(back_recv, back_rs, groups - 1, 0)
+    settle_group(back_recv, back_rs, 0, 1)
+    gather_up(groups - 1, spread2)
+    gather_up(0, spread3)
 
     for half in range(2):
         here = slice(half * 128, half * 128 + 128)
@@ -631,6 +641,7 @@
             pltpu.VMEM((devices, 3, 4, 128), BF16),
             pltpu.VMEM((devices, 3, 4, 128), BF16),
             pltpu.VMEM((256, G * 256), BF16),
+            pltpu.VMEM((256, G * 256), BF16),
             pltpu.VMEM((128, 128), F32),
             pltpu.VMEM((256, 256), F32),
             dma((8,)),

time: 50.5 us -> 49.5 us (0.980)
  Pallas kernels: 49.7 us -> 48.6 us
    pallas_call x1, Pallas kernels: 47.9 us -> 46.9 us  [on_device(): pl.pallas_call(functools.partial(kernel, grps, tiles), out_shape=shapes,...]
where the time goes in v6:
time: 49.5 us; the launch traced here: 49.3 us
  Pallas kernels  48.6 us (98%)
  between operations  0.64 us (1%)
    pallas_call x1, Pallas kernels, on_device(): pl.pallas_call(functools.partial(kernel, grps, tiles), out_shape=shapes,...  46.9 us
    pallas_call x1, Pallas kernels, on_device(): pl.pallas_call(hand_over, out_shape=shapes, in_specs=[far] * 3, out_specs...  1.75 us

profile of v6, /device:TPU:1, one launch (start us, length us, event | category | flops | bytes accessed | tf_op | source)
XLA Modules:
  0.0 49.3 jit_solution(17797223620860971765)
XLA Ops:
  0.6 46.9 %shard_map.148 = (f32[16,16,256]{2,1,0:T(8,128)}, f32[8,1024]{1,0:T(8,128)}, f32[6,16,256]{2,1,0:T(8,128)}) custom-call(f32[16,16,256]{2,1,0:T(8,128)} %atmos_in.1, f32[16,256]{1,0:T(8,128)} %kappa_in.1, s32[16,256]{1,0:T(8,128)} %sea_atm_in.1, f32[12,16]{1,0:T(8,128)} %flux_w.1, s32[1,128]{1,0:T(1,128)} %bitcast.4, s32[1,128]{1,0:T(1,128)} %bitcast.5, ...), custom_call_target="tpu_custom_call" | custom-call | tf_op jit(solution)/shard_map/pallas_call | solution.py:604
  47.5 1.7 %shard_map.149 = (f32[16,16,256]{2,1,0:T(8,128)}, f32[8,1024]{1,0:T(8,128)}, f32[6,16,256]{2,1,0:T(8,128)}) custom-call(f32[16,16,256]{2,1,0:T(8,128)} %get-tuple-element.6.a, f32[8,1024]{1,0:T(8,128)} %get-tuple-element.7.b, f32[6,16,256]{2,1,0:T(8,128)} %get-tuple-element.8.c), custom_call_target="tpu_custom_call" | custom-call | tf_op jit(solution)/shard_map/pallas_call | solution.py:676

commit v7 on v6

--- a/solution.py
+++ b/solution.py
@@ -81,6 +81,7 @@
     fwd_send,
     fwd_recv,
     spread,
+    spread1,
     surf32,
     back_send,
     back_recv,
@@ -433,8 +434,7 @@
 
     total[...] = jnp.zeros_like(total)
 
-    def collect(i, first):
-        settle_group(fwd_recv, fwd_rs, i, first)
+    def collect(i, spread):
         for j in range(G):
             high = dst_hi[i * G + j]
             ends = fwd_recv[i * G + j, 2].astype(F32)
@@ -454,7 +454,17 @@
             preferred_element_type=F32,
         )
 
-    each_group(collect)
+    @pl.loop(0, groups // 2 - 1)
+    def _(n):
+        settle_group(fwd_recv, fwd_rs, 2 * n + 1, 0)
+        settle_group(fwd_recv, fwd_rs, 2 * n + 2, 0)
+        collect(2 * n + 1, spread)
+        collect(2 * n + 2, spread1)
+
+    settle_group(fwd_recv, fwd_rs, groups - 1, 0)
+    settle_group(fwd_recv, fwd_rs, 0, 1)
+    collect(groups - 1, spread)
+    collect(0, spread1)
 
     surf32[...] = jnp.zeros_like(surf32)
     for h in range(8):
@@ -637,6 +647,7 @@
             pltpu.VMEM((devices, 3, 8, 128), BF16),
             pltpu.VMEM((devices, 3, 8, 128), BF16),
             pltpu.VMEM((128, G * 256), BF16),
+            pltpu.VMEM((128, G * 256), BF16),
             pltpu.VMEM((64, 128), F32),
             pltpu.VMEM((devices, 3, 4, 128), BF16),
             pltpu.VMEM((devices, 3, 4, 128), BF16),

time: 49.5 us -> 49 us (0.990)
  Pallas kernels: 48.6 us -> 48.1 us
    pallas_call x1, Pallas kernels: 46.9 us -> 46.4 us  [on_device(): pl.pallas_call(functools.partial(kernel, grps, tiles), out_shape=shapes,...]
where the time goes in v7:
time: 49 us; the launch traced here: 48.8 us
  Pallas kernels  48.1 us (98%)
  between operations  0.64 us (1%)
    pallas_call x1, Pallas kernels, on_device(): pl.pallas_call(functools.partial(kernel, grps, tiles), out_shape=shapes,...  46.4 us
    pallas_call x1, Pallas kernels, on_device(): pl.pallas_call(hand_over, out_shape=shapes, in_specs=[far] * 3, out_specs...  1.75 us

profile of v7, /device:TPU:1, one launch (start us, length us, event | category | flops | bytes accessed | tf_op | source)
XLA Modules:
  0.0 48.8 jit_solution(17463315682539629579)
XLA Ops:
  0.6 46.4 %shard_map.148 = (f32[16,16,256]{2,1,0:T(8,128)}, f32[8,1024]{1,0:T(8,128)}, f32[6,16,256]{2,1,0:T(8,128)}) custom-call(f32[16,16,256]{2,1,0:T(8,128)} %atmos_in.1, f32[16,256]{1,0:T(8,128)} %kappa_in.1, s32[16,256]{1,0:T(8,128)} %sea_atm_in.1, f32[12,16]{1,0:T(8,128)} %flux_w.1, s32[1,128]{1,0:T(1,128)} %bitcast.4, s32[1,128]{1,0:T(1,128)} %bitcast.5, ...), custom_call_target="tpu_custom_call" | custom-call | tf_op jit(solution)/shard_map/pallas_call | solution.py:614
  47.0 1.7 %shard_map.149 = (f32[16,16,256]{2,1,0:T(8,128)}, f32[8,1024]{1,0:T(8,128)}, f32[6,16,256]{2,1,0:T(8,128)}) custom-call(f32[16,16,256]{2,1,0:T(8,128)} %get-tuple-element.6.a, f32[8,1024]{1,0:T(8,128)} %get-tuple-element.7.b, f32[6,16,256]{2,1,0:T(8,128)} %get-tuple-element.8.c), custom_call_target="tpu_custom_call" | custom-call | tf_op jit(solution)/shard_map/pallas_call | solution.py:687
